TPU v7x, 128 devices: a whole 4x4x4 slice. The times are simulated.
128 devices in a mesh: row: 32 (over z, y, core), col: 4 (over x).
Axes of the slice: x: 4, y: 4, z: 4, core: 2. Of those that a mesh axis runs over, the one named last changes fastest.
Arguments:
- tokens: bfloat16 [16384, 2048], P('row', 'col'), may hold values from -6 to 6
- cotangent: bfloat16 [16384, 2048], P('row', 'col'), may hold values from -6 to 6
- destination: int32 [16384], P('row'), may hold values from 0 to 16383, as said below
- segment_ids: int32 [16384], P('row'), may hold values from 0 to 7, as said below
- attn_gain: float32 [2048], replicated, may hold values from 0.5 to 1.5
- w_query: bfloat16 [2048, 2048], P('row', 'col'), may hold values from -0.125 to 0.125
- w_key: bfloat16 [2048, 256], P('row', 'col'), may hold values from -0.125 to 0.125
- w_value: bfloat16 [2048, 256], P('row', 'col'), may hold values from -0.125 to 0.125
- w_output: bfloat16 [2048, 2048], P('row', 'col'), may hold values from -0.5 to 0.5
- ffn_gain: float32 [2048], replicated, may hold values from 0.5 to 1.5
- w_gate: bfloat16 [2048, 5632], P('row', 'col'), may hold values from -0.125 to 0.125
- w_up: bfloat16 [2048, 5632], P('row', 'col'), may hold values from -0.125 to 0.125
- w_down: bfloat16 [2048, 5632], P('row', 'col'), may hold values from -0.078125 to 0.078125
Outputs:
- output: bfloat16 [16384, 2048], P('row', 'col')
- input_grad: bfloat16 [16384, 2048], P('row', 'col')
- attn_gain_grad: float32 [2048], P('row')
- w_query_grad: float32 [2048, 2048], P('row', 'col')
- w_key_grad: float32 [2048, 256], P('row', 'col')
- w_value_grad: float32 [2048, 256], P('row', 'col')
- w_output_grad: float32 [2048, 2048], P('row', 'col')
- ffn_gain_grad: float32 [2048], P('row')
- w_gate_grad: float32 [2048, 5632], P('row', 'col')
- w_up_grad: float32 [2048, 5632], P('row', 'col')
- w_down_grad: float32 [2048, 5632], P('row', 'col')
Inputs may be any that keep to these rules, and one draw needn't show every extreme that they name: `destination`: A permutation; the tokens of each aligned block of 512 arriving tokens go to exactly 16 places in each aligned block of 512 balanced places. `segment_ids`: within each aligned block of 512 places the ids start at 0 and rise by one where a new sequence begins, so a block holds at most 8 sequences; in every draw some block holds a single sequence of 512 tokens and some block holds 8 sequences.
All inputs are finite; a program needn't handle non-finite values.
Results may differ from a plain program's by a relative error of at most 0.028.
Values may be sent and summed in bfloat16 or wider, within the bound.
No kernel may reach another device: no remote copies, remote signals or barrier semaphores. Data moves between devices by JAX's collectives and lax.ppermute only.
A program may use at most 128 MiB of HBM per device.

v0:
```python
from functools import partial

import jax
import jax.numpy as jnp
from jax import lax
from jax.experimental import pallas as pl
from jax.experimental.pallas import tpu as pltpu
from jax.sharding import PartitionSpec as P

HEADS = 32
KV = 4
HD = 64


EPS = 1e-05
ROPE_BASE = 10000.0


def rope_tables(positions):
    half_width = HD // 2
    freqs = ROPE_BASE ** (-(jnp.arange(half_width, dtype=jnp.float32) * 2.0 / HD))
    angles = positions.astype(jnp.float32)[:, None] * freqs[None, :]
    return (jnp.cos(angles)[:, None, :], jnp.sin(angles)[:, None, :])


def rotate(values, cosine, sine):
    half_width = values.shape[-1] // 2
    first = values[..., :half_width]
    second = values[..., half_width:]
    return jnp.concatenate(
        [first * cosine - second * sine, second * cosine + first * sine], axis=-1
    )


def rotate_back(grads, cosine, sine):
    half_width = grads.shape[-1] // 2
    first = grads[..., :half_width]
    second = grads[..., half_width:]
    return jnp.concatenate(
        [first * cosine + second * sine, second * cosine - first * sine], axis=-1
    )


def positions_of(segment_ids):
    index = jnp.arange(segment_ids.shape[0], dtype=jnp.int32)
    change = jnp.concatenate([jnp.ones((1,), dtype=jnp.bool_), segment_ids[1:] != segment_ids[:-1]])
    starts = jnp.where(change, index, jnp.zeros_like(index))
    return index - lax.cummax(starts, axis=0)


def allowed_pairs(segment_ids):
    index = jnp.arange(segment_ids.shape[0], dtype=jnp.int32)
    return (segment_ids[:, None] == segment_ids[None, :]) & (index[None, :] <= index[:, None])


def rms_scale(values):
    return lax.rsqrt(jnp.mean(values * values, axis=-1, keepdims=True) + EPS)


def norm_back(values, inv_root, gain, grads):
    normed = values * inv_root
    scaled = grads * gain
    result = inv_root * (scaled - normed * jnp.mean(scaled * normed, axis=-1, keepdims=True))
    return (result, jnp.sum(grads * normed, axis=0))


def matmul(left, right):
    return jnp.dot(left, right, preferred_element_type=jnp.float32)


def head_scores(query_head, key_head, allowed, scale_factor):
    scores = matmul(query_head, key_head.T) * scale_factor
    return jnp.where(allowed, scores, -1e30)


def head_forward(inputs, key_heads, value_heads, allowed, scale_factor):
    query_head, kv_slot = inputs
    scores = head_scores(query_head, key_heads[kv_slot], allowed, scale_factor)
    peak = jnp.max(scores, axis=-1, keepdims=True)
    expo = jnp.exp(scores - peak)
    total = jnp.sum(expo, axis=-1, keepdims=True)
    probs = expo / total
    mixed = matmul(probs.astype(jnp.bfloat16), value_heads[kv_slot])
    return (mixed, (peak + jnp.log(total))[:, 0])


def head_backward(inputs, key_heads, value_heads, allowed, scale_factor):
    query_head, kv_slot, grad_head, log_total = inputs
    key_head = key_heads[kv_slot]
    value_head = value_heads[kv_slot]
    scores = head_scores(query_head, key_head, allowed, scale_factor)
    probs = jnp.exp(scores - log_total[:, None])
    prob_grad = matmul(grad_head, value_head.T)
    value_grad = matmul(probs.astype(jnp.bfloat16).T, grad_head)
    inner = jnp.sum(probs * prob_grad, axis=-1, keepdims=True)
    score_grad = (probs * (prob_grad - inner)).astype(jnp.bfloat16)
    query_grad = matmul(score_grad, key_head) * scale_factor
    key_grad = matmul(score_grad.T, query_head) * scale_factor
    return (query_grad, key_grad, value_grad)


def grouped(heads, kv_count):
    return heads.reshape(kv_count, heads.shape[0] // kv_count, *heads.shape[1:])


def group_scores(query_groups, key_heads, allowed, scale_factor):
    scores = (
        jnp.einsum("kgqd,kpd->kgqp", query_groups, key_heads, preferred_element_type=jnp.float32)
        * scale_factor
    )
    return jnp.where(allowed, scores, -1e30)


def attention_forward(query_heads, key_heads, value_heads, allowed, scale_factor):
    query_groups = grouped(query_heads, key_heads.shape[0])
    scores = group_scores(query_groups, key_heads, allowed, scale_factor)
    peak = jnp.max(scores, axis=-1, keepdims=True)
    expo = jnp.exp(scores - peak)
    total = jnp.sum(expo, axis=-1, keepdims=True)
    probs = expo / total
    mixed = jnp.einsum(
        "kgqp,kpd->kgqd", probs.astype(jnp.bfloat16), value_heads, preferred_element_type=jnp.float32
    )
    return mixed.reshape(query_heads.shape), (peak + jnp.log(total))[..., 0]


def attention_backward(
    query_heads, key_heads, value_heads, grad_heads, log_totals, allowed, scale_factor
):
    kv_count = key_heads.shape[0]
    query_groups = grouped(query_heads, kv_count)
    grad_groups = grouped(grad_heads, kv_count)
    scores = group_scores(query_groups, key_heads, allowed, scale_factor)
    probs = jnp.exp(scores - log_totals[..., None])
    prob_grad = jnp.einsum(
        "kgqd,kpd->kgqp", grad_groups, value_heads, preferred_element_type=jnp.float32
    )
    value_grad = jnp.einsum(
        "kgqp,kgqd->kpd", probs.astype(jnp.bfloat16), grad_groups, preferred_element_type=jnp.float32
    )
    inner = jnp.sum(probs * prob_grad, axis=-1, keepdims=True)
    score_grad = (probs * (prob_grad - inner)).astype(jnp.bfloat16)
    query_grad = (
        jnp.einsum("kgqp,kpd->kgqd", score_grad, key_heads, preferred_element_type=jnp.float32)
        * scale_factor
    )
    key_grad = (
        jnp.einsum("kgqp,kgqd->kpd", score_grad, query_groups, preferred_element_type=jnp.float32)
        * scale_factor
    )
    return query_grad.reshape(query_heads.shape), key_grad, value_grad


def row_scatter_sum(vectors):
    count = lax.axis_size("row")
    blocks = jnp.moveaxis(vectors.reshape(vectors.shape[0], count, -1), 1, 0)
    return jnp.sum(lax.all_to_all(blocks, "row", split_axis=0, concat_axis=0, tiled=True), axis=0)


GRAD_BLOCK = 128


def split_columns(packed, widths):
    pieces = []
    offset = 0
    for width in widths:
        pieces.append(packed[:, offset : offset + width])
        offset += width
    return pieces


def col_scatter(values):
    count = lax.axis_size("col")
    lead = values.shape[:-1]
    blocks = jnp.moveaxis(values.reshape(*lead, count, values.shape[-1] // count), -2, 0)
    received = lax.all_to_all(blocks, "col", split_axis=0, concat_axis=0, tiled=True)
    return jnp.sum(received.astype(jnp.float32), axis=0)


def col_gather(block):
    count = lax.axis_size("col")
    copies = jnp.broadcast_to(block[None], (count,) + block.shape)
    received = lax.all_to_all(copies, "col", split_axis=0, concat_axis=0, tiled=True)
    return jnp.moveaxis(received, 0, -2).reshape(*block.shape[:-1], count * block.shape[-1])


def col_sum(values):
    return col_gather(col_scatter(values).astype(jnp.bfloat16)).astype(jnp.float32)


def gather_rows(parts):
    return lax.all_gather(jnp.concatenate(parts, axis=1), "row", axis=0, tiled=True)


def grad_wide_kernel(select_ref, left_ref, right_ref, out_ref):
    step = pl.program_id(0)
    parts = out_ref.shape[1] // GRAD_BLOCK
    for part in range(parts):
        owner = select_ref[step * parts + part]
        columns = slice(part * GRAD_BLOCK, (part + 1) * GRAD_BLOCK)
        out_ref[:, columns] = jnp.dot(
            left_ref[owner], right_ref[:, columns], preferred_element_type=jnp.float32
        ).astype(out_ref.dtype)


def packed_weight_grads(lefts, segments):
    left_stack = jnp.stack([left.T for left in lefts])
    right = jnp.concatenate([seg for _, seg in segments], axis=1)
    column_owner = []
    for index, seg in segments:
        column_owner += [index] * seg.shape[1]
    assert len(column_owner) % GRAD_BLOCK == 0
    select = column_owner[::GRAD_BLOCK]
    assert column_owner == [owner for owner in select for _ in range(GRAD_BLOCK)]
    parts = next(m for m in (4, 3, 2, 1) if len(select) % m == 0)
    width = parts * GRAD_BLOCK
    features, tokens = left_stack.shape[1], left_stack.shape[2]
    in_specs = [
        pl.BlockSpec(left_stack.shape, lambda j, sel: (0, 0, 0)),
        pl.BlockSpec((tokens, width), lambda j, sel: (0, j)),
    ]
    return pl.pallas_call(
        grad_wide_kernel,
        out_shape=jax.ShapeDtypeStruct((features, right.shape[1]), jnp.bfloat16),
        grid_spec=pltpu.PrefetchScalarGridSpec(
            num_scalar_prefetch=1,
            grid=(len(select) // parts,),
            in_specs=in_specs,
            out_specs=pl.BlockSpec((features, width), lambda j, sel: (0, j)),
        ),
    )(jnp.asarray(select, dtype=jnp.int32), left_stack, right)


def body(
    tokens,
    cotangent,
    destination,
    segment_ids,
    attn_gain,
    w_query,
    w_key,
    w_value,
    w_output,
    ffn_gain,
    w_gate,
    w_up,
    w_down,
):
    row_count = tokens.shape[0]
    quarter = tokens.shape[1]
    col_start = lax.axis_index("col") * quarter
    send_order = jnp.argsort(destination)
    slot_ids = destination[send_order] % row_count
    arrived_pair, arrived_slots = (
        lax.all_to_all(
            jnp.stack([tokens, cotangent])[:, send_order], "row", split_axis=1, concat_axis=1, tiled=True
        ),
        lax.all_to_all(slot_ids, "row", split_axis=0, concat_axis=0, tiled=True),
    )
    placing = jnp.argsort(arrived_slots)
    attn_widths = [w_query.shape[1], w_key.shape[1], w_value.shape[1], w_output.shape[1]]
    ffn_widths = [w_gate.shape[1], w_up.shape[1], w_down.shape[1]]
    weights_packed = gather_rows([w_query, w_key, w_value, w_output, w_gate, w_up, w_down])
    attn_packed = weights_packed[:, : sum(attn_widths)]
    ffn_packed = weights_packed[:, sum(attn_widths) :]
    placed_pair = arrived_pair[:, placing]
    full_rows = col_gather(placed_pair[0])
    full_grads = col_gather(placed_pair[1])
    query_w, key_w, value_w, output_w = split_columns(attn_packed, attn_widths)
    cosine, sine = rope_tables(positions_of(segment_ids))
    allowed = allowed_pairs(segment_ids)
    rows_wide = full_rows.astype(jnp.float32)
    inv_one = rms_scale(rows_wide)
    normed_one = (rows_wide * inv_one * attn_gain).astype(jnp.bfloat16)
    query = matmul(normed_one, query_w)
    key_raw = matmul(normed_one, key_w)
    value_raw = matmul(normed_one, value_w)
    query_heads_count = query.shape[1] // HD
    kv_count = key_raw.shape[1] // HD
    query_rot = (
        rotate(query.reshape(row_count, query_heads_count, HD), cosine, sine)
        .astype(jnp.bfloat16)
        .transpose(1, 0, 2)
    )
    key_rot = (
        rotate(key_raw.reshape(row_count, kv_count, HD), cosine, sine)
        .astype(jnp.bfloat16)
        .transpose(1, 0, 2)
    )
    value_heads = value_raw.astype(jnp.bfloat16).reshape(row_count, kv_count, HD).transpose(1, 0, 2)
    scale_factor = HD ** (-0.5)
    mixed_heads, log_totals = attention_forward(
        query_rot, key_rot, value_heads, allowed, scale_factor
    )
    mixed = (
        mixed_heads.transpose(1, 0, 2)
        .reshape(row_count, query_heads_count * HD)
        .astype(jnp.bfloat16)
    )
    attn_terms = matmul(mixed, output_w.T)
    attn_full = lax.psum(attn_terms.astype(jnp.bfloat16), "col").astype(jnp.float32)
    resid = rows_wide + attn_full
    inv_two = rms_scale(resid)
    normed_two = (resid * inv_two * ffn_gain).astype(jnp.bfloat16)
    resid_part = lax.dynamic_slice_in_dim(resid, col_start, quarter, 1)
    gate_w, up_w, down_w = split_columns(ffn_packed, ffn_widths)
    gate = matmul(normed_two, gate_w)
    upper = matmul(normed_two, up_w)
    sigmoid_gate = jax.nn.sigmoid(gate)
    activ = (gate * sigmoid_gate * upper).astype(jnp.bfloat16)
    ffn_share_low = lax.psum_scatter(
        matmul(activ, down_w.T).astype(jnp.bfloat16), "col", scatter_dimension=1, tiled=True
    )
    act_grad = matmul(full_grads, down_w)
    gate_grad = (act_grad * upper * sigmoid_gate * (1.0 + gate * (1.0 - sigmoid_gate))).astype(
        jnp.bfloat16
    )
    up_grad = (act_grad * gate * sigmoid_gate).astype(jnp.bfloat16)
    normed_terms_two = matmul(gate_grad, gate_w.T) + matmul(up_grad, up_w.T)
    ffn_grads_packed = packed_weight_grads(
        [normed_two, full_grads], [(0, gate_grad), (0, up_grad), (1, activ)]
    )
    ffn_grads_packed, ffn_share_low = lax.optimization_barrier((ffn_grads_packed, ffn_share_low))
    normed_low_two, ffn_grads_packed = lax.optimization_barrier(
        (normed_terms_two.astype(jnp.bfloat16), ffn_grads_packed)
    )
    normed_grad_two = col_sum(normed_low_two)
    resid_norm_grad, ffn_gain_grad = norm_back(resid, inv_two, ffn_gain, normed_grad_two)
    ffn_grads_local = lax.psum_scatter(ffn_grads_packed, "row", scatter_dimension=0, tiled=True)
    resid_grad = full_grads.astype(jnp.float32) + resid_norm_grad
    attn_grad_low = resid_grad.astype(jnp.bfloat16)
    mixed_grad = matmul(attn_grad_low, output_w).astype(jnp.bfloat16)
    mixed_grad_heads = mixed_grad.reshape(row_count, query_heads_count, HD).transpose(1, 0, 2)
    query_grads, key_grads, value_grads = attention_backward(
        query_rot, key_rot, value_heads, mixed_grad_heads, log_totals, allowed, scale_factor
    )
    query_grad = (
        rotate_back(query_grads.transpose(1, 0, 2), cosine, sine)
        .reshape(row_count, query_heads_count * HD)
        .astype(jnp.bfloat16)
    )
    key_sum = key_grads.transpose(1, 0, 2)
    key_grad = (
        rotate_back(key_sum, cosine, sine).reshape(row_count, kv_count * HD).astype(jnp.bfloat16)
    )
    value_sum = value_grads.transpose(1, 0, 2)
    value_grad = value_sum.reshape(row_count, kv_count * HD).astype(jnp.bfloat16)
    normed_terms_one = (
        matmul(query_grad, query_w.T) + matmul(key_grad, key_w.T) + matmul(value_grad, value_w.T)
    )
    output_share = (resid_part + ffn_share_low.astype(jnp.float32)).astype(jnp.bfloat16)
    back_rows = lax.all_to_all(
        output_share[arrived_slots], "row", split_axis=0, concat_axis=0, tiled=True
    )
    attn_grads_packed, ffn_grads_local, back_rows, normed_low_one = lax.optimization_barrier(
        (
            packed_weight_grads(
                [normed_one, attn_grad_low],
                [(0, query_grad), (0, key_grad), (0, value_grad), (1, mixed)],
            ),
            ffn_grads_local,
            back_rows,
            normed_terms_one.astype(jnp.bfloat16),
        )
    )
    attn_grads_local = lax.psum_scatter(attn_grads_packed, "row", scatter_dimension=0, tiled=True)
    normed_grad_one = col_sum(normed_low_one)
    rows_norm_grad, attn_gain_grad = norm_back(rows_wide, inv_one, attn_gain, normed_grad_one)
    rows_grad = resid_grad + rows_norm_grad
    input_share = lax.dynamic_slice_in_dim(rows_grad, col_start, quarter, 1).astype(jnp.bfloat16)
    query_result, key_result, value_result, output_result = split_columns(
        attn_grads_local.astype(jnp.float32), attn_widths
    )
    gate_result, up_result, down_result = split_columns(
        ffn_grads_local.astype(jnp.float32), ffn_widths
    )
    row_devices = lax.axis_size("row")
    gains = jnp.stack([attn_gain_grad, ffn_gain_grad])
    gain_blocks = jnp.moveaxis(gains.reshape(2, row_devices, -1), 1, 0).reshape(row_devices, -1)
    gain_width = gain_blocks.shape[1]
    assert gain_width <= quarter
    gain_rows = jnp.pad(gain_blocks, ((0, 0), (0, quarter - gain_width)))[:, None, :]
    token_rows = input_share[arrived_slots].reshape(row_devices, -1, quarter)
    received = lax.all_to_all(
        jnp.concatenate([token_rows, gain_rows.astype(jnp.bfloat16)], axis=1),
        "row",
        split_axis=0,
        concat_axis=0,
        tiled=True,
    )
    back_grads = received[:, :-1].reshape(row_count, quarter)
    gain_sums = jnp.sum(received[:, -1, :gain_width].astype(jnp.float32), axis=0).reshape(2, -1)
    attn_gain_result, ffn_gain_result = gain_sums[0], gain_sums[1]
    restore = jnp.argsort(send_order)
    return (
        back_rows[restore],
        back_grads[restore],
        attn_gain_result,
        query_result,
        key_result,
        value_result,
        output_result,
        ffn_gain_result,
        gate_result,
        up_result,
        down_result,
    )

def solution(mesh):
    placed = (
        P("row", "col"),
        P("row", "col"),
        P("row"),
        P("row"),
        P(),
        P("row", "col"),
        P("row", "col"),
        P("row", "col"),
        P("row", "col"),
        P(),
        P("row", "col"),
        P("row", "col"),
        P("row", "col"),
    )
    return jax.shard_map(
        body,
        mesh=mesh,
        in_specs=placed,
        out_specs=(
            P("row", "col"),
            P("row", "col"),
            P("row"),
            P("row", "col"),
            P("row", "col"),
            P("row", "col"),
            P("row", "col"),
            P("row"),
            P("row", "col"),
            P("row", "col"),
            P("row", "col"),
        ),
        check_vma=False,
    )
```

profile of v0, /device:TPU:1, one launch (start us, length us, event | category | flops | bytes accessed | tf_op | source)
XLA Modules:
  0.0 521.0 jit_solution(14992776955670761920)
XLA Ops:
  7.2 2.1 concatenate.44
  9.4 4.4 sort.45
  14.4 3.6 gather_fusion.1
  18.7 9.6 %all-to-all-start.1 = ((s32[32,16,1]{1,2,0:T(1,128)}), s32[32,16,1]{1,2,0:T(1,128)S(1)}, u32[]{:S(2)}, u32[]{:S(2)}) async-start(s32[32,16,1]{1,2,0:T(1,128)} %bitcast.3), calls=%async_computation.1 | async-start | bytes 32768 | tf_op jit(solution)/shard_map/all_to_all | solution.py:258
  30.0 2.4 pad_maximum_fusion.3
  32.4 4.1 gather_fusion
  36.6 7.4 %all-to-all-start = ((bf16[2,512,512]{2,0,1:T(2,128)(2,1)}), bf16[2,512,512]{2,0,1:T(2,128)(2,1)S(1)}, u32[]{:S(2)}, u32[]{:S(2)}) async-start(bf16[2,512,512]{2,0,1:T(2,128)(2,1)} %bitcast.2), calls=%async_computation | async-start | bytes 2097152 | tf_op jit(solution)/shard_map/all_to_all | solution.py:255
  45.2 3.8 sort.46
  49.0 17.1 %all-to-all-done = bf16[2,512,512]{2,0,1:T(2,128)(2,1)S(1)} async-done(((bf16[2,512,512]{2,0,1:T(2,128)(2,1)}), bf16[2,512,512]{2,0,1:T(2,128)(2,1)S(1)}, u32[]{:S(2)}, u32[]{:S(2)}) %all-to-all-start) | async-done | bytes 1048608 | tf_op jit(solution)/shard_map/all_to_all | solution.py:255
  66.2 3.6 gather_fusion.2
  74.1 4.0 all-to-all-start.2
  81.1 2.3 copy.161
  83.4 19.5 %all-to-all-done.2 = bf16[4,512,512]{1,2,0:T(8,128)(2,1)S(1)} async-done(((bf16[4,512,512]{1,2,0:T(8,128)(2,1)}), bf16[4,512,512]{1,2,0:T(8,128)(2,1)S(1)}, u32[]{:S(2)}, u32[]{:S(2)}) %all-to-all-start.2) | async-done | bytes 2097184 | tf_op jit(solution)/shard_map/all_to_all | solution.py:183
  102.9 2.5 broadcast_in_dim.33
  105.4 4.4 all-to-all-start.3
  110.7 1.9 fusion.25
  112.6 3.1 bitcast_multiply_fusion.5
  115.7 3.1 slice_bitcast_fusion
  118.7 4.0 copy.124
  122.7 2.4 convolution_bitcast_fusion.1
  126.4 3.6 fusion.94
  132.9 2.0 copy-done.3
  134.9 2.1 fusion.52
  139.4 4.2 convolution_convert_fusion
  144.1 8.3 %fusion.12 = f32[512,1408]{1,0:T(8,128)} fusion(bf16[512,2048]{0,1:T(8,128)(2,1)} %bitcast.12, bf16[2048,5376]{1,0:T(8,128)(2,1)} %all-gather.2.cloned.1.call-done), kind=kOutput, calls=%fused_computation.25 | convolution fusion | flops 2952790016 | bytes 10747904 | tf_op jit(solution)/shard_map/dot_general | solution.py:68
  152.4 51.4 %all-reduce.3.cloned.1.call-done = bf16[512,2048]{0,1:T(8,128)(2,1)} async-done(((bf16[512,2048]{0,1:T(8,128)(2,1)}), bf16[512,2048]{0,1:T(8,128)(2,1)}) %all-reduce.3.cloned.1.call-update) | async-done | bytes 2097168 | tf_op jit(solution)/shard_map/psum | solution.py:301
  203.8 2.5 multiply_reduce_fusion.1
  207.1 6.4 %fusion.4 = f32[512,1408]{1,0:T(8,128)S(1)} fusion(bf16[512,2048]{0,1:T(8,128)(2,1)S(1)} %multiply_convert_fusion.1, bf16[2048,5376]{1,0:T(8,128)(2,1)} %all-gather.2.cloned.1.call-done), kind=kOutput, calls=%fused_computation.17 | convolution fusion | flops 2952790016 | bytes 10747904 | tf_op jit(solution)/shard_map/dot_general | solution.py:68
  213.6 9.0 %multiply_convert_fusion.3 = (bf16[512,1408]{1,0:T(8,128)(2,1)S(1)}, bf16[512,1408]{1,0:T(8,128)(2,1)}, bf16[512,1408]{1,0:T(8,128)(2,1)S(1)}) fusion(f32[512,1408]{1,0:T(8,128)S(1)} %fusion.4, f32[512,1408]{1,0:T(8,128)S(1)} %copy-done.51, bf16[512,2048]{0,1:T(8,128)(2,1)S(1)} %multiply_convert_fusion.1, bf16[2048,5376]{1,0:T(8,128)(2,1)} %all-gather.2.cloned.1.call-done), kind=kOutput, calls=%fused_computation.60 | convolution fusion | flops 2964324352 | bytes 17956864 | tf_op jit(solution)/shard_map/dot_general | solution.py:68
  223.7 7.3 %fusion.31 = bf16[512,2048]{0,1:T(8,128)(2,1)} fusion(bf16[512,1408]{1,0:T(8,128)(2,1)S(1)} %get-tuple-element.39, bf16[2048,5376]{1,0:T(8,128)(2,1)} %all-gather.2.cloned.1.call-done), kind=kOutput, calls=%fused_computation.59 | convolution fusion | flops 2953838592 | bytes 9306112 | tf_op jit(solution)/shard_map/dot_general | solution.py:68
  231.3 4.7 pad_maximum_fusion.1.left_ref
  236.1 2.1 pad_maximum_fusion.right_ref
  238.2 24.6 %shard_map.230 = bf16[2048,4224]{1,0:T(8,128)(2,1)} custom-call(s32[33]{0:T(128)} %constant.67.clone.select_ref, bf16[2,2048,512]{2,1,0:T(8,128)(2,1)} %pad_maximum_fusion.1.left_ref, bf16[512,4224]{1,0:T(8,128)(2,1)} %pad_maximum_fusion.right_ref), custom_call_target="tpu_custom_call" | custom-call | tf_op jit(solution)/shard_map/pallas_call | solution.py:222
  262.8 5.9 %fusion.2 = f32[512,2048]{1,0:T(8,128)S(1)} fusion(bf16[512,1408]{1,0:T(8,128)(2,1)} %get-tuple-element.40, bf16[2048,5376]{1,0:T(8,128)(2,1)} %all-gather.2.cloned.1.call-done), kind=kOutput, calls=%fused_computation.15 | convolution fusion | flops 2952790016 | bytes 11403264 | tf_op jit(solution)/shard_map/dot_general | solution.py:68
  268.7 7.5 %add_convert_fusion.1 = bf16[512,2048]{1,0:T(8,128)(2,1)} fusion(f32[512,2048]{1,0:T(8,128)S(1)} %fusion.2, bf16[512,1408]{1,0:T(8,128)(2,1)S(1)} %get-tuple-element.41, bf16[2048,5376]{1,0:T(8,128)(2,1)} %all-gather.2.cloned.1.call-done), kind=kOutput, calls=%fused_computation.53 | convolution fusion | flops 2954887168 | bytes 13500416 | tf_op jit(solution)/shard_map/dot_general | solution.py:68
  278.0 28.7 %all_to_all.64 = bf16[4,512,512]{2,1,0:T(8,128)(2,1)} all-to-all(bf16[4,512,512]{2,1,0:T(8,128)(2,1)S(1)} %bitcast.189), channel_id=1, replica_groups=mesh['row'=32,'col'=4] {'col'}, dimensions={0} | all-to-all | bytes 4194304 | tf_op jit(solution)/shard_map/all_to_all | solution.py:176
  306.8 2.4 reduce_sum.108
  311.0 4.6 all-to-all-start.5
  316.7 23.6 %all-to-all-done.5 = bf16[4,512,512]{1,2,0:T(8,128)(2,1)} async-done(((bf16[4,512,512]{1,2,0:T(8,128)(2,1)}), bf16[4,512,512]{1,2,0:T(8,128)(2,1)}, u32[]{:S(2)}, u32[]{:S(2)}) %all-to-all-start.5) | async-done | bytes 2097184 | tf_op jit(solution)/shard_map/all_to_all | solution.py:183
  340.3 3.7 fusion.21
  344.4 2.6 gather_fusion.3
  347.0 9.4 %all-to-all-start.6 = ((bf16[32,16,512]{2,1,0:T(8,128)(2,1)}), bf16[32,16,512]{2,1,0:T(8,128)(2,1)S(1)}, u32[]{:S(2)}, u32[]{:S(2)}) async-start(bf16[32,16,512]{2,1,0:T(8,128)(2,1)} %bitcast.51), calls=%async_computation.8 | async-start | bytes 1048576 | tf_op jit(solution)/shard_map/all_to_all | solution.py:352
  356.6 4.1 convert_bitcast_fusion
  360.8 5.0 fusion.40
  365.8 2.5 multiply_reduce_fusion
  368.3 2.6 multiply_convert_fusion
  374.8 3.9 fusion.58
  378.7 4.9 fusion.34
  385.2 2.4 pad_maximum_fusion.2.left_ref
  388.5 3.2 concatenate.54.right_ref
  391.7 9.9 %shard_map.231 = bf16[2048,1152]{1,0:T(8,128)(2,1)} custom-call(s32[9]{0:T(128)} %constant.68.clone.select_ref, bf16[2,2048,512]{2,1,0:T(8,128)(2,1)} %pad_maximum_fusion.2.left_ref, bf16[512,1152]{1,0:T(8,128)(2,1)} %concatenate.54.right_ref), custom_call_target="tpu_custom_call" | custom-call | tf_op jit(solution)/shard_map/pallas_call | solution.py:222
  401.6 5.7 %add_convert_fusion = bf16[512,2048]{1,0:T(8,128)(2,1)} fusion(f32[512,2048]{1,0:T(8,128)} %fusion.34, f32[512,2048]{1,0:T(8,128)} %fusion.58, bf16[512,64]{1,0:T(8,128)(2,1)S(1)} %fusion.49, bf16[2048,5376]{1,0:T(8,128)(2,1)} %all-gather.2.cloned.1.call-done), kind=kOutput, calls=%fused_computation.51 | convolution fusion | flops 137363456 | bytes 11075584 | tf_op jit(solution)/shard_map/dot_general | solution.py:68
  409.2 29.3 %all_to_all.65 = bf16[4,512,512]{2,1,0:T(8,128)(2,1)} all-to-all(bf16[4,512,512]{2,1,0:T(8,128)(2,1)S(1)} %bitcast.190), channel_id=1, replica_groups=mesh['row'=32,'col'=4] {'col'}, dimensions={0} | all-to-all | bytes 4194304 | tf_op jit(solution)/shard_map/all_to_all | solution.py:176
  438.5 2.9 reduce_sum.111
  444.2 4.4 all-to-all-start.8
  449.4 3.8 sort.47
  453.3 20.6 %all-to-all-done.8 = bf16[4,512,512]{1,2,0:T(8,128)(2,1)} async-done(((bf16[4,512,512]{1,2,0:T(8,128)(2,1)}), bf16[4,512,512]{1,2,0:T(8,128)(2,1)}, u32[]{:S(2)}, u32[]{:S(2)}) %all-to-all-start.8) | async-done | bytes 2097184 | tf_op jit(solution)/shard_map/all_to_all | solution.py:183
  473.8 2.9 fusion.24
  477.0 2.2 convert_element_type.211
  481.3 2.0 gather_fusion.5
  484.3 9.1 %all-to-all-start.9 = ((bf16[32,17,512]{2,1,0:T(8,128)(2,1)}), bf16[32,17,512]{2,1,0:T(8,128)(2,1)S(1)}, u32[]{:S(2)}, u32[]{:S(2)}) async-start(bf16[32,17,512]{2,1,0:T(8,128)(2,1)} %pad_maximum_fusion.4), calls=%async_computation.11 | async-start | bytes 1572864 | tf_op jit(solution)/shard_map/all_to_all | solution.py:384
  493.4 2.6 gather_fusion.4
  497.1 10.6 %all-to-all-done.9 = bf16[32,17,512]{2,1,0:T(8,128)(2,1)S(1)} async-done(((bf16[32,17,512]{2,1,0:T(8,128)(2,1)}), bf16[32,17,512]{2,1,0:T(8,128)(2,1)S(1)}, u32[]{:S(2)}, u32[]{:S(2)}) %all-to-all-start.9) | async-done | bytes 557088 | tf_op jit(solution)/shard_map/all_to_all | solution.py:384
  507.7 2.6 gather_fusion.6
  (204 shorter events, 46.5 us)
Async XLA Ops:
  7.2 21.2 %copy-start.22 = (bf16[512,512]{1,0:T(8,128)(2,1)S(1)}, bf16[512,512]{1,0:T(8,128)(2,1)}, u32[]{:S(2)}) copy-start(bf16[512,512]{1,0:T(8,128)(2,1)} %param.15) | copy-start | bytes 1572868
  7.2 22.0 %copy-start.23 = (bf16[512,512]{1,0:T(8,128)(2,1)S(1)}, bf16[512,512]{1,0:T(8,128)(2,1)}, u32[]{:S(2)}) copy-start(bf16[512,512]{1,0:T(8,128)(2,1)} %param.16) | copy-start | bytes 1572868
  7.2 108.5 %all-gather.2.cloned.1.call-start = ((), (), s32[]{:S(2)}) async-start(), calls=%async_computation.13 | async-start | bytes 22708224 | tf_op jit(solution)/shard_map/all_gather | solution.py:192
  18.7 17.8 %all-to-all-start.1 = ((s32[32,16,1]{1,2,0:T(1,128)}), s32[32,16,1]{1,2,0:T(1,128)S(1)}, u32[]{:S(2)}, u32[]{:S(2)}) async-start(s32[32,16,1]{1,2,0:T(1,128)} %bitcast.3), calls=%async_computation.1 | async-start | bytes 32768 | tf_op jit(solution)/shard_map/all_to_all | solution.py:258
  36.6 33.2 %copy-start.27 = (s32[32,16,1]{1,2,0:T(1,128)}, s32[32,16,1]{1,2,0:T(1,128)S(1)}, u32[]{:S(2)}) copy-start(s32[32,16,1]{1,2,0:T(1,128)S(1)} %all-to-all-done.1) | copy-start | bytes 6148
  36.6 29.6 %all-to-all-start = ((bf16[2,512,512]{2,0,1:T(2,128)(2,1)}), bf16[2,512,512]{2,0,1:T(2,128)(2,1)S(1)}, u32[]{:S(2)}, u32[]{:S(2)}) async-start(bf16[2,512,512]{2,0,1:T(2,128)(2,1)} %bitcast.2), calls=%async_computation | async-start | bytes 2097152 | tf_op jit(solution)/shard_map/all_to_all | solution.py:255
  71.3 6.9 %copy-start.43 = (s32[512]{0:T(512)S(1)}, s32[512]{0:T(512)}, u32[]{:S(2)}) copy-start(s32[512]{0:T(512)} %param.18) | copy-start | bytes 6148
  71.3 7.4 %copy-start.39 = (f32[2048]{0:T(1024)S(1)}, f32[2048]{0:T(1024)}, u32[]{:S(2)}) copy-start(f32[2048]{0:T(1024)} %param.19) | copy-start | bytes 24580
  74.1 28.8 %all-to-all-start.2 = ((bf16[4,512,512]{1,2,0:T(8,128)(2,1)}), bf16[4,512,512]{1,2,0:T(8,128)(2,1)S(1)}, u32[]{:S(2)}, u32[]{:S(2)}) async-start(bf16[4,512,512]{1,2,0:T(8,128)(2,1)} %broadcast_in_dim.31), calls=%async_computation.2 | async-start | bytes 4194304 | tf_op jit(solution)/shard_map/all_to_all | solution.py:183
  78.7 31.9 %copy-start.31 = (f32[4,512]{1,0:T(4,128)}, f32[4,512]{1,0:T(4,128)S(1)}, u32[]{:S(2)}) copy-start(f32[4,512]{1,0:T(4,128)S(1)} %mul.299) | copy-start | bytes 24580
  80.2 49.8 %copy-start.18 = (f32[512,32]{0,1:T(8,128)}, f32[512,32]{0,1:T(8,128)S(1)}, u32[]{:S(2)}) copy-start(f32[512,32]{0,1:T(8,128)S(1)} %get-tuple-element.62) | copy-start | bytes 196612
  80.2 49.8 %copy-start.20 = (f32[512,32]{0,1:T(8,128)}, f32[512,32]{0,1:T(8,128)S(1)}, u32[]{:S(2)}) copy-start(f32[512,32]{0,1:T(8,128)S(1)} %get-tuple-element.63) | copy-start | bytes 196612
  105.4 38.7 %all-to-all-start.3 = ((bf16[4,512,512]{1,2,0:T(8,128)(2,1)}), bf16[4,512,512]{1,2,0:T(8,128)(2,1)}, u32[]{:S(2)}, u32[]{:S(2)}) async-start(bf16[4,512,512]{1,2,0:T(8,128)(2,1)} %broadcast_in_dim.33), calls=%async_computation.3 | async-start | bytes 4194304 | tf_op jit(solution)/shard_map/all_to_all | solution.py:183
  109.9 93.9 %all-reduce.3.cloned.1.call-start = ((), (), s32[]{:S(2)}) async-start(), calls=%async_computation.14 | async-start | bytes 4194304 | tf_op jit(solution)/shard_map/psum | solution.py:301
  110.6 5.0 copy-start.37
  118.7 6.4 %copy-start.41 = (f32[512]{0:T(512)S(1)}, f32[512]{0:T(512)}, u32[]{:S(2)}) copy-start(f32[512]{0:T(512)} %copy-done.40) | copy-start | bytes 6148
  118.7 6.4 %copy-start.49 = (f32[32]{0:T(128)S(1)}, f32[32]{0:T(128)}, u32[]{:S(2)}) copy-start(f32[32]{0:T(128)} %copy-done.48) | copy-start | bytes 388
  126.4 3.8 copy-start.10
  126.4 3.8 copy-start.12
  130.2 1.5 copy-start.14
  130.2 1.5 copy-start.16
  131.7 5.3 %copy-start = (f32[8,512,512]{1,2,0:T(8,128)}, f32[8,512,512]{1,2,0:T(8,128)S(1)}, u32[]{:S(2)}) copy-start(f32[8,512,512]{1,2,0:T(8,128)S(1)} %get-tuple-element.67) | copy-start | bytes 25165828
  131.7 3.2 copy-start.3
  134.9 3.7 copy-start.35
  137.0 1.6 copy-start.33
  138.6 0.8 copy-start.25
  143.6 132.6 %reduce-scatter.4.cloned.1.call-start = ((), (), s32[]{:S(2)}) async-start(), calls=%async_computation.15 | async-start | bytes 2621440 | tf_op jit(solution)/shard_map/reduce_scatter | solution.py:311
  152.4 53.9 %copy-start.29 = (f32[2048]{0:T(1024)S(1)}, f32[2048]{0:T(1024)}, u32[]{:S(2)}) copy-start(f32[2048]{0:T(1024)} %param.24) | copy-start | bytes 24580
  203.8 2.5 copy-start.1
  206.3 0.8 copy-start.44
  207.1 6.4 %copy-start.2 = (bf16[512,2048]{0,1:T(8,128)(2,1)}, bf16[512,2048]{0,1:T(8,128)(2,1)S(1)}, u32[]{:S(2)}) copy-start(bf16[512,2048]{0,1:T(8,128)(2,1)S(1)} %multiply_convert_fusion.1) | copy-start | bytes 6291460
  207.1 6.4 %copy-start.51 = (f32[512,1408]{1,0:T(8,128)S(1)}, f32[512,1408]{1,0:T(8,128)}, u32[]{:S(2)}) copy-start(f32[512,1408]{1,0:T(8,128)} %fusion.12) | copy-start | bytes 8650756
  222.6 1.1 copy-start.8
  231.1 176.3 %reduce-scatter.6.cloned.1.call-start = ((), (), s32[]{:S(2)}) async-start(), calls=%async_computation.16 | async-start | bytes 17842176 | tf_op jit(solution)/shard_map/reduce_scatter | solution.py:329
  231.3 4.8 copy-start.7
  231.3 4.8 copy-start.9
  309.2 6.4 %copy-start.28 = (s32[32,16,1]{1,2,0:T(1,128)S(1)}, s32[32,16,1]{1,2,0:T(1,128)}, u32[]{:S(2)}) copy-start(s32[32,16,1]{1,2,0:T(1,128)} %copy-done.27) | copy-start | bytes 6148
  309.4 6.2 %copy-start.26 = (bf16[8,512,64]{1,2,0:T(8,128)(2,1)S(1)}, bf16[8,512,64]{1,2,0:T(8,128)(2,1)}, u32[]{:S(2)}) copy-start(bf16[8,512,64]{1,2,0:T(8,128)(2,1)} %copy-done.25) | copy-start | bytes 1572868
  309.4 7.3 %copy-start.36 = (f32[8,512]{1,0:T(8,128)S(1)}, f32[8,512]{1,0:T(8,128)}, u32[]{:S(2)}) copy-start(f32[8,512]{1,0:T(8,128)} %copy-done.35) | copy-start | bytes 49156
  309.5 30.8 %copy-start.30 = (f32[2048]{0:T(1024)S(1)}, f32[2048]{0:T(1024)}, u32[]{:S(2)}) copy-start(f32[2048]{0:T(1024)} %param.24) | copy-start | bytes 24580
  309.5 30.8 %copy-start.45 = (f32[512]{0:T(512)S(1)}, f32[512]{0:T(512)}, u32[]{:S(2)}) copy-start(f32[512]{0:T(512)} %copy-done.44) | copy-start | bytes 6148
  311.0 29.3 %all-to-all-start.5 = ((bf16[4,512,512]{1,2,0:T(8,128)(2,1)}), bf16[4,512,512]{1,2,0:T(8,128)(2,1)}, u32[]{:S(2)}, u32[]{:S(2)}) async-start(bf16[4,512,512]{1,2,0:T(8,128)(2,1)} %broadcast_in_dim.36), calls=%async_computation.6 | async-start | bytes 4194304 | tf_op jit(solution)/shard_map/all_to_all | solution.py:183
  316.7 27.3 %copy-start.24 = (bf16[512,512]{0,1:T(8,128)(2,1)S(1)}, bf16[512,512]{0,1:T(8,128)(2,1)}, u32[]{:S(2)}) copy-start(bf16[512,512]{0,1:T(8,128)(2,1)} %reduce-scatter.4.cloned.1.call-done) | copy-start | bytes 1572868
  347.0 60.3 %all-to-all-start.6 = ((bf16[32,16,512]{2,1,0:T(8,128)(2,1)}), bf16[32,16,512]{2,1,0:T(8,128)(2,1)S(1)}, u32[]{:S(2)}, u32[]{:S(2)}) async-start(bf16[32,16,512]{2,1,0:T(8,128)(2,1)} %bitcast.51), calls=%async_computation.8 | async-start | bytes 1048576 | tf_op jit(solution)/shard_map/all_to_all | solution.py:352
  356.5 154.5 %reduce-scatter.8.cloned.1.call-start = ((), (), s32[]{:S(2)}) async-start(), calls=%async_computation.17 | async-start | bytes 4866048 | tf_op jit(solution)/shard_map/reduce_scatter | solution.py:366
  356.6 9.2 %slice-start = ((s8[8388608]{0:T(1024)(128)(4,1)}), s8[4194304]{0:T(1024)(128)(4,1)S(1)}, s32[]{:S(2)}) async-start(s8[8388608]{0:T(1024)(128)(4,1)} %bitcast.183), calls=%async_computation.18 | async-start | bytes 8388608
  356.6 9.2 %slice-start.1 = ((s8[8388608]{0:T(1024)(128)(4,1)}), s8[4194304]{0:T(1024)(128)(4,1)S(1)}, s32[]{:S(2)}) async-start(s8[8388608]{0:T(1024)(128)(4,1)} %bitcast.183), calls=%async_computation.19 | async-start | bytes 8388608
  360.7 5.0 copy-start.5
  360.7 5.0 copy-start.34
  368.3 2.6 copy-start.15
  368.3 2.6 copy-start.17
  370.9 1.3 copy-start.42
  370.9 1.3 copy-start.50
  370.9 2.6 copy-start.11
  370.9 2.6 copy-start.13
  372.2 2.4 copy-start.19
  372.2 2.4 copy-start.21
  383.6 1.6 copy-start.4
  441.4 8.0 %copy-start.47 = (s32[512]{0:T(512)S(1)}, s32[512]{0:T(512)}, u32[]{:S(2)}) copy-start(s32[512]{0:T(512)} %copy-done.46) | copy-start | bytes 6148
  441.4 32.4 %copy-start.32 = (f32[4,512]{1,0:T(4,128)S(1)}, f32[4,512]{1,0:T(4,128)}, u32[]{:S(2)}) copy-start(f32[4,512]{1,0:T(4,128)} %copy-done.31) | copy-start | bytes 24580
  441.4 32.4 %copy-start.38 = (f32[512]{0:T(512)S(1)}, f32[512]{0:T(512)}, u32[]{:S(2)}) copy-start(f32[512]{0:T(512)} %copy-done.37) | copy-start | bytes 6148
  444.2 29.6 %all-to-all-start.8 = ((bf16[4,512,512]{1,2,0:T(8,128)(2,1)}), bf16[4,512,512]{1,2,0:T(8,128)(2,1)}, u32[]{:S(2)}, u32[]{:S(2)}) async-start(bf16[4,512,512]{1,2,0:T(8,128)(2,1)} %broadcast_in_dim.38), calls=%async_computation.10 | async-start | bytes 4194304 | tf_op jit(solution)/shard_map/all_to_all | solution.py:183
  483.3 12.8 %copy-start.6 = (bf16[64,4224]{1,0:T(8,128)(2,1)S(1)}, bf16[64,4224]{1,0:T(8,128)(2,1)}, u32[]{:S(2)}) copy-start(bf16[64,4224]{1,0:T(8,128)(2,1)} %reduce-scatter.6.cloned.1.call-done) | copy-start | bytes 1622020
  484.3 23.4 %all-to-all-start.9 = ((bf16[32,17,512]{2,1,0:T(8,128)(2,1)}), bf16[32,17,512]{2,1,0:T(8,128)(2,1)S(1)}, u32[]{:S(2)}, u32[]{:S(2)}) async-start(bf16[32,17,512]{2,1,0:T(8,128)(2,1)} %pad_maximum_fusion.4), calls=%async_computation.11 | async-start | bytes 1572864 | tf_op jit(solution)/shard_map/all_to_all | solution.py:384
  (3 other events, 1.7 us)
Sparse Core Ops, SparseCore 0:
  10.3 95.7 all-gather.1
  143.7 60.0 all-reduce.2
  231.2 29.5 reduce-scatter.3
  276.4 121.2 reduce-scatter.5
  407.5 81.2 reduce-scatter.7
where the time goes:
time: 531 us; the launch traced here: 521 us
  waiting for transfers between devices  143 us (27%)
  matrix products  85.2 us (16%)
  local copies, waits for them, and re-layouts  67.4 us (13%)
  other arithmetic  63.7 us (12%)
  blocking collectives  58 us (11%)
  starting transfers between devices  54 us (10%)
  Pallas kernels  34.5 us (6%)
  between operations  15.3 us (3%)
    dot_general x14, matrix products, matmul(): return jnp.dot(left, right, preferred_element_type=jnp.float32)  76.3 us
    all_to_all x4, waiting for transfers between devices, col_gather(): lax.all_to_all(copies, 'col', split_axis=0, concat_axis=0, tiled=True)  63.6 us
    all_to_all x2, blocking collectives, col_scatter(): lax.all_to_all(blocks, 'col', split_axis=0, concat_axis=0, tiled=True)  58 us
    psum x1, waiting for transfers between devices, body(): lax.psum(attn_terms.astype(jnp.bfloat16), 'col').astype(jnp.float32)  51.4 us
    pallas_call x2, Pallas kernels, packed_weight_grads(): pl.pallas_call(grad_wide_kernel, out_shape=jax.ShapeDtypeStruct((features...  34.5 us
    all_to_all x4, starting transfers between devices, col_gather(): lax.all_to_all(copies, 'col', split_axis=0, concat_axis=0, tiled=True)  17.5 us
    all_to_all x1, waiting for transfers between devices, body(): lax.all_to_all(jnp.stack([tokens, cotangent])[:, send_order], 'row', spli...  17.1 us
    another operation x3, other arithmetic, packed_weight_grads(): left_stack = jnp.stack([left.T for left in lefts])  11.3 us
  transfers between devices with their start and end apart: 13, of which 6 were waited for; matrix products, arithmetic and copies ran while one was open for 34% of the time, Pallas kernels for 7%

commit v1 on v0

--- a/solution.py
+++ b/solution.py
@@ -364,10 +364,20 @@
         )
     )
     attn_grads_local = lax.psum_scatter(attn_grads_packed, "row", scatter_dimension=0, tiled=True)
-    normed_grad_one = col_sum(normed_low_one)
-    rows_norm_grad, attn_gain_grad = norm_back(rows_wide, inv_one, attn_gain, normed_grad_one)
-    rows_grad = resid_grad + rows_norm_grad
-    input_share = lax.dynamic_slice_in_dim(rows_grad, col_start, quarter, 1).astype(jnp.bfloat16)
+    normed_grad_block = col_scatter(normed_low_one)
+    normed_block = lax.dynamic_slice_in_dim(rows_wide, col_start, quarter, 1) * inv_one
+    scaled_block = normed_grad_block * lax.dynamic_slice_in_dim(attn_gain, col_start, quarter, 0)
+    token_part = jnp.sum(scaled_block * normed_block, axis=-1)
+    gain_part = jnp.sum(normed_grad_block * normed_block, axis=0)
+    exchanged = col_gather(jnp.concatenate([token_part, gain_part])).reshape(
+        -1, token_part.shape[0] + gain_part.shape[0]
+    )
+    row_mean = jnp.sum(exchanged[:, : token_part.shape[0]], axis=0) / rows_wide.shape[-1]
+    attn_gain_grad = exchanged[:, token_part.shape[0] :].reshape(-1)
+    input_block = lax.dynamic_slice_in_dim(resid_grad, col_start, quarter, 1) + inv_one * (
+        scaled_block - normed_block * row_mean[:, None]
+    )
+    input_share = input_block.astype(jnp.bfloat16)
     query_result, key_result, value_result, output_result = split_columns(
         attn_grads_local.astype(jnp.float32), attn_widths
     )

time: 531 us -> 508 us (0.957)
  the two profiles are of different devices: /device:TPU:1 before, /device:TPU:0 now
where the time goes in v1:
time: 508 us; the launch traced here: 498 us
  waiting for transfers between devices  152 us (30%)
  matrix products  84.6 us (17%)
  local copies, waits for them, and re-layouts  67 us (13%)
  other arithmetic  62.5 us (12%)
  starting transfers between devices  52.6 us (10%)
  Pallas kernels  34.4 us (7%)
  blocking collectives  29.9 us (6%)
  between operations  15.3 us (3%)
    dot_general x14, matrix products, matmul(): return jnp.dot(left, right, preferred_element_type=jnp.float32)  75.7 us
    psum x1, waiting for transfers between devices, body(): lax.psum(attn_terms.astype(jnp.bfloat16), 'col').astype(jnp.float32)  49.5 us
    all_to_all x4, waiting for transfers between devices, col_gather(): lax.all_to_all(copies, 'col', split_axis=0, concat_axis=0, tiled=True)  46.4 us
    pallas_call x2, Pallas kernels, packed_weight_grads(): pl.pallas_call(grad_wide_kernel, out_shape=jax.ShapeDtypeStruct((features...  34.4 us
    all_to_all x1, blocking collectives, col_scatter(): lax.all_to_all(blocks, 'col', split_axis=0, concat_axis=0, tiled=True)  29.9 us
    all_to_all x1, waiting for transfers between devices, col_scatter(): lax.all_to_all(blocks, 'col', split_axis=0, concat_axis=0, tiled=True)  19.9 us
    all_to_all x1, waiting for transfers between devices, body(): lax.all_to_all(jnp.stack([tokens, cotangent])[:, send_order], 'row', spli...  18.2 us
    all_to_all x4, starting transfers between devices, col_gather(): lax.all_to_all(copies, 'col', split_axis=0, concat_axis=0, tiled=True)  16.7 us
  transfers between devices with their start and end apart: 14, of which 8 were waited for; matrix products, arithmetic and copies ran while one was open for 35% of the time, Pallas kernels for 7%

profile of v1, /device:TPU:0, one launch (start us, length us, event | category | flops | bytes accessed | tf_op | source)
XLA Modules:
  0.0 497.9 jit_solution(6803523625712557883)
XLA Ops:
  7.2 2.1 concatenate.47
  9.4 4.4 sort.45
  14.4 3.6 gather_fusion.1
  18.7 8.4 %all-to-all-start.1 = ((s32[32,16,1]{1,2,0:T(1,128)}), s32[32,16,1]{1,2,0:T(1,128)S(1)}, u32[]{:S(2)}, u32[]{:S(2)}) async-start(s32[32,16,1]{1,2,0:T(1,128)} %bitcast.3), calls=%async_computation.1 | async-start | bytes 32768 | tf_op jit(solution)/shard_map/all_to_all | solution.py:258
  28.8 2.4 pad_maximum_fusion.3
  31.3 4.1 gather_fusion
  35.4 7.4 %all-to-all-start = ((bf16[2,512,512]{2,0,1:T(2,128)(2,1)}), bf16[2,512,512]{2,0,1:T(2,128)(2,1)S(1)}, u32[]{:S(2)}, u32[]{:S(2)}) async-start(bf16[2,512,512]{2,0,1:T(2,128)(2,1)} %bitcast.2), calls=%async_computation | async-start | bytes 2097152 | tf_op jit(solution)/shard_map/all_to_all | solution.py:255
  44.1 3.8 sort.46
  47.9 18.2 %all-to-all-done = bf16[2,512,512]{2,0,1:T(2,128)(2,1)S(1)} async-done(((bf16[2,512,512]{2,0,1:T(2,128)(2,1)}), bf16[2,512,512]{2,0,1:T(2,128)(2,1)S(1)}, u32[]{:S(2)}, u32[]{:S(2)}) %all-to-all-start) | async-done | bytes 1048608 | tf_op jit(solution)/shard_map/all_to_all | solution.py:255
  66.1 3.6 gather_fusion.2
  74.0 4.3 all-to-all-start.2
  80.6 2.3 copy.163
  82.9 21.2 %all-to-all-done.2 = bf16[4,512,512]{1,2,0:T(8,128)(2,1)S(1)} async-done(((bf16[4,512,512]{1,2,0:T(8,128)(2,1)}), bf16[4,512,512]{1,2,0:T(8,128)(2,1)S(1)}, u32[]{:S(2)}, u32[]{:S(2)}) %all-to-all-start.2) | async-done | bytes 2097184 | tf_op jit(solution)/shard_map/all_to_all | solution.py:183
  104.0 2.6 broadcast_in_dim.33
  106.6 4.4 all-to-all-start.3
  115.5 2.4 convolution_bitcast_fusion.1
  119.2 3.1 slice_bitcast_fusion
  122.3 4.0 copy.125
  126.3 3.5 fusion.86
  134.6 2.1 fusion.47
  139.1 4.1 convolution_convert_fusion
  143.8 8.3 %fusion.12 = f32[512,1408]{1,0:T(8,128)} fusion(bf16[512,2048]{0,1:T(8,128)(2,1)} %bitcast.12, bf16[2048,5376]{1,0:T(8,128)(2,1)} %all-gather.2.cloned.1.call-done), kind=kOutput, calls=%fused_computation.25 | convolution fusion | flops 2952790016 | bytes 10747904 | tf_op jit(solution)/shard_map/dot_general | solution.py:68
  152.1 49.5 %all-reduce.3.cloned.1.call-done = bf16[512,2048]{0,1:T(8,128)(2,1)} async-done(((bf16[512,2048]{0,1:T(8,128)(2,1)}), bf16[512,2048]{0,1:T(8,128)(2,1)}) %all-reduce.3.cloned.1.call-update) | async-done | bytes 2097168 | tf_op jit(solution)/shard_map/psum | solution.py:301
  201.7 2.5 multiply_reduce_fusion.1
  204.2 2.7 convert_add_fusion
  206.9 6.4 %fusion.4 = f32[512,1408]{1,0:T(8,128)S(1)} fusion(bf16[512,2048]{0,1:T(8,128)(2,1)S(1)} %get-tuple-element.43, bf16[2048,5376]{1,0:T(8,128)(2,1)} %all-gather.2.cloned.1.call-done), kind=kOutput, calls=%fused_computation.17 | convolution fusion | flops 2952790016 | bytes 10747904 | tf_op jit(solution)/shard_map/dot_general | solution.py:68
  213.4 8.9 %multiply_convert_fusion.4 = (bf16[512,1408]{1,0:T(8,128)(2,1)S(1)}, bf16[512,1408]{1,0:T(8,128)(2,1)}, bf16[512,1408]{1,0:T(8,128)(2,1)S(1)}) fusion(f32[512,1408]{1,0:T(8,128)S(1)} %fusion.4, f32[512,1408]{1,0:T(8,128)S(1)} %copy-done.50, bf16[512,2048]{0,1:T(8,128)(2,1)S(1)} %get-tuple-element.43, bf16[2048,5376]{1,0:T(8,128)(2,1)} %all-gather.2.cloned.1.call-done), kind=kOutput, calls=%fused_computation.52 | convolution fusion | flops 2964324352 | bytes 17956864 | tf_op jit(solution)/shard_map/dot_general | solution.py:68
  223.4 7.3 %fusion.26 = bf16[512,2048]{0,1:T(8,128)(2,1)} fusion(bf16[512,1408]{1,0:T(8,128)(2,1)S(1)} %get-tuple-element.39, bf16[2048,5376]{1,0:T(8,128)(2,1)} %all-gather.2.cloned.1.call-done), kind=kOutput, calls=%fused_computation.51 | convolution fusion | flops 2953838592 | bytes 9306112 | tf_op jit(solution)/shard_map/dot_general | solution.py:68
  231.0 4.7 pad_maximum_fusion.1.left_ref
  235.7 2.1 pad_maximum_fusion.right_ref
  237.8 24.4 %shard_map.230 = bf16[2048,4224]{1,0:T(8,128)(2,1)} custom-call(s32[33]{0:T(128)} %constant.67.clone.select_ref, bf16[2,2048,512]{2,1,0:T(8,128)(2,1)} %pad_maximum_fusion.1.left_ref, bf16[512,4224]{1,0:T(8,128)(2,1)} %pad_maximum_fusion.right_ref), custom_call_target="tpu_custom_call" | custom-call | tf_op jit(solution)/shard_map/pallas_call | solution.py:222
  262.3 5.9 %fusion.2 = f32[512,2048]{1,0:T(8,128)S(1)} fusion(bf16[512,1408]{1,0:T(8,128)(2,1)} %get-tuple-element.40, bf16[2048,5376]{1,0:T(8,128)(2,1)} %all-gather.2.cloned.1.call-done), kind=kOutput, calls=%fused_computation.15 | convolution fusion | flops 2952790016 | bytes 11403264 | tf_op jit(solution)/shard_map/dot_general | solution.py:68
  268.2 7.4 %add_convert_fusion.1 = bf16[512,2048]{1,0:T(8,128)(2,1)} fusion(f32[512,2048]{1,0:T(8,128)S(1)} %fusion.2, bf16[512,1408]{1,0:T(8,128)(2,1)S(1)} %get-tuple-element.41, bf16[2048,5376]{1,0:T(8,128)(2,1)} %all-gather.2.cloned.1.call-done), kind=kOutput, calls=%fused_computation.42 | convolution fusion | flops 2954887168 | bytes 13500416 | tf_op jit(solution)/shard_map/dot_general | solution.py:68
  277.4 29.9 %all_to_all.68 = bf16[4,512,512]{2,1,0:T(8,128)(2,1)} all-to-all(bf16[4,512,512]{2,1,0:T(8,128)(2,1)S(1)} %bitcast.178), channel_id=1, replica_groups=mesh['row'=32,'col'=4] {'col'}, dimensions={0} | all-to-all | bytes 4194304 | tf_op jit(solution)/shard_map/all_to_all | solution.py:176
  307.3 2.4 reduce_sum.114
  311.5 4.7 all-to-all-start.5
  319.0 2.6 gather_fusion.3
  321.6 20.1 %all-to-all-done.5 = bf16[4,512,512]{1,2,0:T(8,128)(2,1)} async-done(((bf16[4,512,512]{1,2,0:T(8,128)(2,1)}), bf16[4,512,512]{1,2,0:T(8,128)(2,1)}, u32[]{:S(2)}, u32[]{:S(2)}) %all-to-all-start.5) | async-done | bytes 2097184 | tf_op jit(solution)/shard_map/all_to_all | solution.py:183
  341.7 7.2 %all-to-all-start.6 = ((bf16[32,16,512]{2,1,0:T(8,128)(2,1)}), bf16[32,16,512]{2,1,0:T(8,128)(2,1)S(1)}, u32[]{:S(2)}, u32[]{:S(2)}) async-start(bf16[32,16,512]{2,1,0:T(8,128)(2,1)} %bitcast.51), calls=%async_computation.8 | async-start | bytes 1048576 | tf_op jit(solution)/shard_map/all_to_all | solution.py:352
  349.2 3.8 fusion.21
  353.1 3.5 convert_bitcast_fusion
  356.6 4.7 fusion.35
  361.4 2.5 multiply_reduce_fusion
  363.9 2.6 multiply_convert_fusion
  370.5 3.8 fusion.50
  374.2 4.9 fusion.29
  380.7 2.5 pad_maximum_fusion.2.left_ref
  384.2 3.1 concatenate.57.right_ref
  387.3 10.0 %shard_map.231 = bf16[2048,1152]{1,0:T(8,128)(2,1)} custom-call(s32[9]{0:T(128)} %constant.68.clone.select_ref, bf16[2,2048,512]{2,1,0:T(8,128)(2,1)} %pad_maximum_fusion.2.left_ref, bf16[512,1152]{1,0:T(8,128)(2,1)} %concatenate.57.right_ref), custom_call_target="tpu_custom_call" | custom-call | tf_op jit(solution)/shard_map/pallas_call | solution.py:222
  397.4 5.8 %add_convert_fusion = bf16[512,2048]{1,0:T(8,128)(2,1)} fusion(f32[512,2048]{1,0:T(8,128)} %fusion.29, f32[512,2048]{1,0:T(8,128)} %fusion.50, bf16[512,64]{1,0:T(8,128)(2,1)S(1)} %fusion.44, bf16[2048,5376]{1,0:T(8,128)(2,1)} %all-gather.2.cloned.1.call-done), kind=kOutput, calls=%fused_computation.40 | convolution fusion | flops 137363456 | bytes 11075584 | tf_op jit(solution)/shard_map/dot_general | solution.py:68
  403.2 3.2 copy.177
  406.3 4.5 all-to-all-start.7
  411.6 3.8 sort.47
  415.3 2.5 convert_element_type.186
  417.9 19.9 %all-to-all-done.7 = bf16[4,512,512]{2,1,0:T(8,128)(2,1)} async-done(((bf16[4,512,512]{2,1,0:T(8,128)(2,1)}), bf16[4,512,512]{2,1,0:T(8,128)(2,1)}, u32[]{:S(2)}, u32[]{:S(2)}) %all-to-all-start.7) | async-done | bytes 2097184 | tf_op jit(solution)/shard_map/all_to_all | solution.py:176
  437.8 2.0 convert_reduce_fusion
  442.4 3.3 all-to-all-start.8
  445.7 5.2 %all-to-all-done.8 = f32[4,1,1024]{2,1,0:T(1,128)S(1)} async-done(((f32[4,1,1024]{2,1,0:T(1,128)}), f32[4,1,1024]{2,1,0:T(1,128)S(1)}, u32[]{:S(2)}, u32[]{:S(2)}) %all-to-all-start.8) | async-done | bytes 16416 | tf_op jit(solution)/shard_map/all_to_all | solution.py:183
  453.1 2.0 gather_fusion.5
  456.3 7.3 %all-to-all-start.9 = ((bf16[32,17,512]{2,1,0:T(8,128)(2,1)}), bf16[32,17,512]{2,1,0:T(8,128)(2,1)S(1)}, u32[]{:S(2)}, u32[]{:S(2)}) async-start(bf16[32,17,512]{2,1,0:T(8,128)(2,1)} %pad_maximum_fusion.4), calls=%async_computation.11 | async-start | bytes 1572864 | tf_op jit(solution)/shard_map/all_to_all | solution.py:394
  463.6 2.6 gather_fusion.4
  467.2 10.9 %all-to-all-done.9 = bf16[32,17,512]{2,1,0:T(8,128)(2,1)S(1)} async-done(((bf16[32,17,512]{2,1,0:T(8,128)(2,1)}), bf16[32,17,512]{2,1,0:T(8,128)(2,1)S(1)}, u32[]{:S(2)}, u32[]{:S(2)}) %all-to-all-start.9) | async-done | bytes 557088 | tf_op jit(solution)/shard_map/all_to_all | solution.py:394
  478.2 2.6 gather_fusion.6
  481.5 6.4 %reduce-scatter.8.cloned.1.call-done = bf16[64,1152]{1,0:T(8,128)(2,1)} async-done(((bf16[2048,1152]{1,0:T(8,128)(2,1)}), bf16[64,1152]{1,0:T(8,128)(2,1)}) %reduce-scatter.8.cloned.1.call-update) | async-done | bytes 147472 | tf_op jit(solution)/shard_map/reduce_scatter | solution.py:366
  (207 shorter events, 50.0 us)
Async XLA Ops:
  7.2 20.0 %copy-start.23 = (bf16[512,512]{1,0:T(8,128)(2,1)S(1)}, bf16[512,512]{1,0:T(8,128)(2,1)}, u32[]{:S(2)}) copy-start(bf16[512,512]{1,0:T(8,128)(2,1)} %param.15) | copy-start | bytes 1572868
  7.2 20.8 %copy-start.24 = (bf16[512,512]{1,0:T(8,128)(2,1)S(1)}, bf16[512,512]{1,0:T(8,128)(2,1)}, u32[]{:S(2)}) copy-start(bf16[512,512]{1,0:T(8,128)(2,1)} %param.16) | copy-start | bytes 1572868
  7.2 108.3 %all-gather.2.cloned.1.call-start = ((), (), s32[]{:S(2)}) async-start(), calls=%async_computation.13 | async-start | bytes 22708224 | tf_op jit(solution)/shard_map/all_gather | solution.py:192
  18.7 16.6 %all-to-all-start.1 = ((s32[32,16,1]{1,2,0:T(1,128)}), s32[32,16,1]{1,2,0:T(1,128)S(1)}, u32[]{:S(2)}, u32[]{:S(2)}) async-start(s32[32,16,1]{1,2,0:T(1,128)} %bitcast.3), calls=%async_computation.1 | async-start | bytes 32768 | tf_op jit(solution)/shard_map/all_to_all | solution.py:258
  35.4 34.3 %copy-start.28 = (s32[32,16,1]{1,2,0:T(1,128)}, s32[32,16,1]{1,2,0:T(1,128)S(1)}, u32[]{:S(2)}) copy-start(s32[32,16,1]{1,2,0:T(1,128)S(1)} %all-to-all-done.1) | copy-start | bytes 6148
  35.4 30.7 %all-to-all-start = ((bf16[2,512,512]{2,0,1:T(2,128)(2,1)}), bf16[2,512,512]{2,0,1:T(2,128)(2,1)S(1)}, u32[]{:S(2)}, u32[]{:S(2)}) async-start(bf16[2,512,512]{2,0,1:T(2,128)(2,1)} %bitcast.2), calls=%async_computation | async-start | bytes 2097152 | tf_op jit(solution)/shard_map/all_to_all | solution.py:255
  71.2 7.2 %copy-start.42 = (s32[512]{0:T(512)S(1)}, s32[512]{0:T(512)}, u32[]{:S(2)}) copy-start(s32[512]{0:T(512)} %param.18) | copy-start | bytes 6148
  71.2 7.7 %copy-start.38 = (f32[2048]{0:T(1024)S(1)}, f32[2048]{0:T(1024)}, u32[]{:S(2)}) copy-start(f32[2048]{0:T(1024)} %param.19) | copy-start | bytes 24580
  74.0 30.0 %all-to-all-start.2 = ((bf16[4,512,512]{1,2,0:T(8,128)(2,1)}), bf16[4,512,512]{1,2,0:T(8,128)(2,1)S(1)}, u32[]{:S(2)}, u32[]{:S(2)}) async-start(bf16[4,512,512]{1,2,0:T(8,128)(2,1)} %broadcast_in_dim.31), calls=%async_computation.2 | async-start | bytes 4194304 | tf_op jit(solution)/shard_map/all_to_all | solution.py:183
  80.0 37.9 %copy-start.39 = (f32[512]{0:T(512)}, f32[512]{0:T(512)S(1)}, u32[]{:S(2)}) copy-start(f32[512]{0:T(512)S(1)} %fusion.75) | copy-start | bytes 6148
  80.3 49.4 %copy-start.19 = (f32[512,32]{0,1:T(8,128)}, f32[512,32]{0,1:T(8,128)S(1)}, u32[]{:S(2)}) copy-start(f32[512,32]{0,1:T(8,128)S(1)} %get-tuple-element.61) | copy-start | bytes 196612
  80.4 49.4 %copy-start.21 = (f32[512,32]{0,1:T(8,128)}, f32[512,32]{0,1:T(8,128)S(1)}, u32[]{:S(2)}) copy-start(f32[512,32]{0,1:T(8,128)S(1)} %get-tuple-element.62) | copy-start | bytes 196612
  104.0 7.8 %copy-start.41 = (f32[4,512]{1,0:T(4,128)S(1)}, f32[4,512]{1,0:T(4,128)}, u32[]{:S(2)}) copy-start(f32[4,512]{1,0:T(4,128)} %mul.298) | copy-start | bytes 24580
  106.6 37.2 %all-to-all-start.3 = ((bf16[4,512,512]{1,2,0:T(8,128)(2,1)}), bf16[4,512,512]{1,2,0:T(8,128)(2,1)}, u32[]{:S(2)}, u32[]{:S(2)}) async-start(bf16[4,512,512]{1,2,0:T(8,128)(2,1)} %broadcast_in_dim.33), calls=%async_computation.3 | async-start | bytes 4194304 | tf_op jit(solution)/shard_map/all_to_all | solution.py:183
  111.0 90.6 %all-reduce.3.cloned.1.call-start = ((), (), s32[]{:S(2)}) async-start(), calls=%async_computation.14 | async-start | bytes 4194304 | tf_op jit(solution)/shard_map/psum | solution.py:301
  111.8 1.9 copy-start.36
  113.7 4.3 copy-start.48
  119.2 10.8 %copy-start.11 = (bf16[512,32]{1,0:T(8,128)(2,1)}, bf16[512,32]{1,0:T(8,128)(2,1)S(1)}, u32[]{:S(2)}) copy-start(bf16[512,32]{1,0:T(8,128)(2,1)S(1)} %get-tuple-element.55) | copy-start | bytes 98308
  119.2 10.8 %copy-start.13 = (bf16[512,32]{1,0:T(8,128)(2,1)}, bf16[512,32]{1,0:T(8,128)(2,1)S(1)}, u32[]{:S(2)}) copy-start(bf16[512,32]{1,0:T(8,128)(2,1)S(1)} %get-tuple-element.56) | copy-start | bytes 98308
  129.9 1.5 copy-start.15
  129.9 1.5 copy-start.17
  131.5 5.3 %copy-start = (f32[8,512,512]{1,2,0:T(8,128)}, f32[8,512,512]{1,2,0:T(8,128)S(1)}, u32[]{:S(2)}) copy-start(f32[8,512,512]{1,2,0:T(8,128)S(1)} %get-tuple-element.66) | copy-start | bytes 25165828
  131.5 3.2 copy-start.4
  134.6 3.7 copy-start.34
  136.8 1.6 copy-start.32
  143.3 132.3 %reduce-scatter.4.cloned.1.call-start = ((), (), s32[]{:S(2)}) async-start(), calls=%async_computation.15 | async-start | bytes 2621440 | tf_op jit(solution)/shard_map/reduce_scatter | solution.py:311
  152.1 52.0 %copy-start.30 = (f32[2048]{0:T(1024)S(1)}, f32[2048]{0:T(1024)}, u32[]{:S(2)}) copy-start(f32[2048]{0:T(1024)} %param.24) | copy-start | bytes 24580
  201.7 2.5 copy-start.1
  204.2 2.7 copy-start.43
  206.9 6.4 %copy-start.3 = (bf16[512,2048]{0,1:T(8,128)(2,1)}, bf16[512,2048]{0,1:T(8,128)(2,1)S(1)}, u32[]{:S(2)}) copy-start(bf16[512,2048]{0,1:T(8,128)(2,1)S(1)} %get-tuple-element.43) | copy-start | bytes 6291460
  206.9 6.4 %copy-start.50 = (f32[512,1408]{1,0:T(8,128)S(1)}, f32[512,1408]{1,0:T(8,128)}, u32[]{:S(2)}) copy-start(f32[512,1408]{1,0:T(8,128)} %fusion.12) | copy-start | bytes 8650756
  222.3 1.1 copy-start.9
  230.7 172.4 %reduce-scatter.6.cloned.1.call-start = ((), (), s32[]{:S(2)}) async-start(), calls=%async_computation.16 | async-start | bytes 17842176 | tf_op jit(solution)/shard_map/reduce_scatter | solution.py:329
  231.0 4.7 copy-start.8
  231.0 4.7 copy-start.10
  309.7 6.4 %copy-start.29 = (s32[32,16,1]{1,2,0:T(1,128)S(1)}, s32[32,16,1]{1,2,0:T(1,128)}, u32[]{:S(2)}) copy-start(s32[32,16,1]{1,2,0:T(1,128)} %copy-done.28) | copy-start | bytes 6148
  309.9 6.3 %copy-start.27 = (bf16[8,512,64]{1,2,0:T(8,128)(2,1)S(1)}, bf16[8,512,64]{1,2,0:T(8,128)(2,1)}, u32[]{:S(2)}) copy-start(bf16[8,512,64]{1,2,0:T(8,128)(2,1)} %copy-done.26) | copy-start | bytes 1572868
  310.0 7.3 %copy-start.35 = (f32[8,512]{1,0:T(8,128)S(1)}, f32[8,512]{1,0:T(8,128)}, u32[]{:S(2)}) copy-start(f32[8,512]{1,0:T(8,128)} %copy-done.34) | copy-start | bytes 49156
  311.5 5.8 %copy-start.25 = (bf16[512,512]{0,1:T(8,128)(2,1)S(1)}, bf16[512,512]{0,1:T(8,128)(2,1)}, u32[]{:S(2)}) copy-start(bf16[512,512]{0,1:T(8,128)(2,1)} %reduce-scatter.4.cloned.1.call-done) | copy-start | bytes 1572868
  311.5 30.2 %all-to-all-start.5 = ((bf16[4,512,512]{1,2,0:T(8,128)(2,1)}), bf16[4,512,512]{1,2,0:T(8,128)(2,1)}, u32[]{:S(2)}, u32[]{:S(2)}) async-start(bf16[4,512,512]{1,2,0:T(8,128)(2,1)} %broadcast_in_dim.36), calls=%async_computation.6 | async-start | bytes 4194304 | tf_op jit(solution)/shard_map/all_to_all | solution.py:183
  317.3 31.9 %copy-start.31 = (f32[2048]{0:T(1024)S(1)}, f32[2048]{0:T(1024)}, u32[]{:S(2)}) copy-start(f32[2048]{0:T(1024)} %param.24) | copy-start | bytes 24580
  317.3 31.9 %copy-start.44 = (f32[512]{0:T(512)S(1)}, f32[512]{0:T(512)}, u32[]{:S(2)}) copy-start(f32[512]{0:T(512)} %copy-done.43) | copy-start | bytes 6148
  341.7 61.5 %all-to-all-start.6 = ((bf16[32,16,512]{2,1,0:T(8,128)(2,1)}), bf16[32,16,512]{2,1,0:T(8,128)(2,1)S(1)}, u32[]{:S(2)}, u32[]{:S(2)}) async-start(bf16[32,16,512]{2,1,0:T(8,128)(2,1)} %bitcast.51), calls=%async_computation.8 | async-start | bytes 1048576 | tf_op jit(solution)/shard_map/all_to_all | solution.py:352
  348.9 138.9 %reduce-scatter.8.cloned.1.call-start = ((), (), s32[]{:S(2)}) async-start(), calls=%async_computation.17 | async-start | bytes 4866048 | tf_op jit(solution)/shard_map/reduce_scatter | solution.py:366
  349.2 3.9 copy-start.2
  353.1 8.3 %slice-start = ((s8[8388608]{0:T(1024)(128)(4,1)}), s8[4194304]{0:T(1024)(128)(4,1)S(1)}, s32[]{:S(2)}) async-start(s8[8388608]{0:T(1024)(128)(4,1)} %bitcast.169), calls=%async_computation.18 | async-start | bytes 8388608
  353.1 8.3 %slice-start.1 = ((s8[8388608]{0:T(1024)(128)(4,1)}), s8[4194304]{0:T(1024)(128)(4,1)S(1)}, s32[]{:S(2)}) async-start(s8[8388608]{0:T(1024)(128)(4,1)} %bitcast.169), calls=%async_computation.19 | async-start | bytes 8388608
  356.6 4.8 copy-start.6
  356.6 4.8 copy-start.33
  363.9 2.6 copy-start.16
  363.9 2.6 copy-start.18
  366.6 1.3 copy-start.40
  366.6 1.3 copy-start.49
  366.6 2.6 copy-start.12
  366.6 2.6 copy-start.14
  367.9 2.4 copy-start.20
  367.9 2.4 copy-start.22
  379.1 1.6 copy-start.5
  403.2 8.4 %copy-start.46 = (s32[512]{0:T(512)S(1)}, s32[512]{0:T(512)}, u32[]{:S(2)}) copy-start(s32[512]{0:T(512)} %copy-done.45) | copy-start | bytes 6148
  406.3 31.5 %all-to-all-start.7 = ((bf16[4,512,512]{2,1,0:T(8,128)(2,1)}), bf16[4,512,512]{2,1,0:T(8,128)(2,1)}, u32[]{:S(2)}, u32[]{:S(2)}) async-start(bf16[4,512,512]{2,1,0:T(8,128)(2,1)} %bitcast.177), calls=%async_computation.9 | async-start | bytes 4194304 | tf_op jit(solution)/shard_map/all_to_all | solution.py:176
  417.9 22.3 %copy-start.37 = (f32[512]{0:T(512)S(1)}, f32[512]{0:T(512)}, u32[]{:S(2)}) copy-start(f32[512]{0:T(512)} %copy-done.36) | copy-start | bytes 6148
  442.4 8.6 %all-to-all-start.8 = ((f32[4,1,1024]{2,1,0:T(1,128)}), f32[4,1,1024]{2,1,0:T(1,128)S(1)}, u32[]{:S(2)}, u32[]{:S(2)}) async-start(f32[4,1,1024]{2,1,0:T(1,128)} %broadcast_in_dim.38), calls=%async_computation.10 | async-start | bytes 32768 | tf_op jit(solution)/shard_map/all_to_all | solution.py:183
  455.0 11.2 %copy-start.7 = (bf16[64,4224]{1,0:T(8,128)(2,1)S(1)}, bf16[64,4224]{1,0:T(8,128)(2,1)}, u32[]{:S(2)}) copy-start(bf16[64,4224]{1,0:T(8,128)(2,1)} %reduce-scatter.6.cloned.1.call-done) | copy-start | bytes 1622020
  456.3 21.8 %all-to-all-start.9 = ((bf16[32,17,512]{2,1,0:T(8,128)(2,1)}), bf16[32,17,512]{2,1,0:T(8,128)(2,1)S(1)}, u32[]{:S(2)}, u32[]{:S(2)}) async-start(bf16[32,17,512]{2,1,0:T(8,128)(2,1)} %pad_maximum_fusion.4), calls=%async_computation.11 | async-start | bytes 1572864 | tf_op jit(solution)/shard_map/all_to_all | solution.py:394
  (3 other events, 1.9 us)
Sparse Core Ops, SparseCore 0:
  10.3 94.5 all-gather.1
  143.4 58.1 all-reduce.2
  230.9 29.4 reduce-scatter.3
  275.7 122.4 reduce-scatter.5
  403.3 84.4 reduce-scatter.7

commit v2 on v1

--- a/solution.py
+++ b/solution.py
@@ -212,7 +212,7 @@
     assert len(column_owner) % GRAD_BLOCK == 0
     select = column_owner[::GRAD_BLOCK]
     assert column_owner == [owner for owner in select for _ in range(GRAD_BLOCK)]
-    parts = next(m for m in (4, 3, 2, 1) if len(select) % m == 0)
+    parts = max(m for m in range(1, 12) if len(select) % m == 0 and len(select) // m >= 3)
     width = parts * GRAD_BLOCK
     features, tokens = left_stack.shape[1], left_stack.shape[2]
     in_specs = [

time: 508 us -> 508 us (level)
  no operation moved by 1% of the time
where the time goes in v2:
time: 508 us; the launch traced here: 498 us
  waiting for transfers between devices  151 us (30%)
  matrix products  84.6 us (17%)
  local copies, waits for them, and re-layouts  67 us (13%)
  other arithmetic  62.5 us (12%)
  starting transfers between devices  52.4 us (10%)
  Pallas kernels  34.7 us (7%)
  blocking collectives  29.9 us (6%)
  between operations  15.3 us (3%)
    dot_general x14, matrix products, matmul(): return jnp.dot(left, right, preferred_element_type=jnp.float32)  75.7 us
    psum x1, waiting for transfers between devices, body(): lax.psum(attn_terms.astype(jnp.bfloat16), 'col').astype(jnp.float32)  49.5 us
    all_to_all x4, waiting for transfers between devices, col_gather(): lax.all_to_all(copies, 'col', split_axis=0, concat_axis=0, tiled=True)  46.6 us
    pallas_call x2, Pallas kernels, packed_weight_grads(): pl.pallas_call(grad_wide_kernel, out_shape=jax.ShapeDtypeStruct((features...  34.7 us
    all_to_all x1, blocking collectives, col_scatter(): lax.all_to_all(blocks, 'col', split_axis=0, concat_axis=0, tiled=True)  29.9 us
    all_to_all x1, waiting for transfers between devices, col_scatter(): lax.all_to_all(blocks, 'col', split_axis=0, concat_axis=0, tiled=True)  19.9 us
    all_to_all x1, waiting for transfers between devices, body(): lax.all_to_all(jnp.stack([tokens, cotangent])[:, send_order], 'row', spli...  18.2 us
    all_to_all x4, starting transfers between devices, col_gather(): lax.all_to_all(copies, 'col', split_axis=0, concat_axis=0, tiled=True)  16.6 us
  transfers between devices with their start and end apart: 14, of which 8 were waited for; matrix products, arithmetic and copies ran while one was open for 35% of the time, Pallas kernels for 7%

profile of v2, /device:TPU:0, one launch (start us, length us, event | category | flops | bytes accessed | tf_op | source)
XLA Modules:
  0.0 497.9 jit_solution(3144050762946439460)
XLA Ops:
  7.2 2.1 concatenate.47
  9.4 4.4 sort.45
  14.4 3.6 gather_fusion.1
  18.7 8.4 %all-to-all-start.1 = ((s32[32,16,1]{1,2,0:T(1,128)}), s32[32,16,1]{1,2,0:T(1,128)S(1)}, u32[]{:S(2)}, u32[]{:S(2)}) async-start(s32[32,16,1]{1,2,0:T(1,128)} %bitcast.3), calls=%async_computation.1 | async-start | bytes 32768 | tf_op jit(solution)/shard_map/all_to_all | solution.py:258
  28.8 2.4 pad_maximum_fusion.3
  31.3 4.1 gather_fusion
  35.4 7.4 %all-to-all-start = ((bf16[2,512,512]{2,0,1:T(2,128)(2,1)}), bf16[2,512,512]{2,0,1:T(2,128)(2,1)S(1)}, u32[]{:S(2)}, u32[]{:S(2)}) async-start(bf16[2,512,512]{2,0,1:T(2,128)(2,1)} %bitcast.2), calls=%async_computation | async-start | bytes 2097152 | tf_op jit(solution)/shard_map/all_to_all | solution.py:255
  44.1 3.8 sort.46
  47.9 18.2 %all-to-all-done = bf16[2,512,512]{2,0,1:T(2,128)(2,1)S(1)} async-done(((bf16[2,512,512]{2,0,1:T(2,128)(2,1)}), bf16[2,512,512]{2,0,1:T(2,128)(2,1)S(1)}, u32[]{:S(2)}, u32[]{:S(2)}) %all-to-all-start) | async-done | bytes 1048608 | tf_op jit(solution)/shard_map/all_to_all | solution.py:255
  66.1 3.6 gather_fusion.2
  74.0 4.3 all-to-all-start.2
  80.6 2.3 copy.163
  82.9 21.2 %all-to-all-done.2 = bf16[4,512,512]{1,2,0:T(8,128)(2,1)S(1)} async-done(((bf16[4,512,512]{1,2,0:T(8,128)(2,1)}), bf16[4,512,512]{1,2,0:T(8,128)(2,1)S(1)}, u32[]{:S(2)}, u32[]{:S(2)}) %all-to-all-start.2) | async-done | bytes 2097184 | tf_op jit(solution)/shard_map/all_to_all | solution.py:183
  104.0 2.6 broadcast_in_dim.33
  106.6 4.4 all-to-all-start.3
  115.5 2.4 convolution_bitcast_fusion.1
  119.2 3.1 slice_bitcast_fusion
  122.3 4.0 copy.125
  126.3 3.5 fusion.86
  134.6 2.1 fusion.47
  139.1 4.1 convolution_convert_fusion
  143.8 8.3 %fusion.12 = f32[512,1408]{1,0:T(8,128)} fusion(bf16[512,2048]{0,1:T(8,128)(2,1)} %bitcast.12, bf16[2048,5376]{1,0:T(8,128)(2,1)} %all-gather.2.cloned.1.call-done), kind=kOutput, calls=%fused_computation.25 | convolution fusion | flops 2952790016 | bytes 10747904 | tf_op jit(solution)/shard_map/dot_general | solution.py:68
  152.1 49.5 %all-reduce.3.cloned.1.call-done = bf16[512,2048]{0,1:T(8,128)(2,1)} async-done(((bf16[512,2048]{0,1:T(8,128)(2,1)}), bf16[512,2048]{0,1:T(8,128)(2,1)}) %all-reduce.3.cloned.1.call-update) | async-done | bytes 2097168 | tf_op jit(solution)/shard_map/psum | solution.py:301
  201.7 2.5 multiply_reduce_fusion.1
  204.2 2.7 convert_add_fusion
  206.9 6.4 %fusion.4 = f32[512,1408]{1,0:T(8,128)S(1)} fusion(bf16[512,2048]{0,1:T(8,128)(2,1)S(1)} %get-tuple-element.43, bf16[2048,5376]{1,0:T(8,128)(2,1)} %all-gather.2.cloned.1.call-done), kind=kOutput, calls=%fused_computation.17 | convolution fusion | flops 2952790016 | bytes 10747904 | tf_op jit(solution)/shard_map/dot_general | solution.py:68
  213.4 8.9 %multiply_convert_fusion.4 = (bf16[512,1408]{1,0:T(8,128)(2,1)S(1)}, bf16[512,1408]{1,0:T(8,128)(2,1)}, bf16[512,1408]{1,0:T(8,128)(2,1)S(1)}) fusion(f32[512,1408]{1,0:T(8,128)S(1)} %fusion.4, f32[512,1408]{1,0:T(8,128)S(1)} %copy-done.50, bf16[512,2048]{0,1:T(8,128)(2,1)S(1)} %get-tuple-element.43, bf16[2048,5376]{1,0:T(8,128)(2,1)} %all-gather.2.cloned.1.call-done), kind=kOutput, calls=%fused_computation.52 | convolution fusion | flops 2964324352 | bytes 17956864 | tf_op jit(solution)/shard_map/dot_general | solution.py:68
  223.4 7.3 %fusion.26 = bf16[512,2048]{0,1:T(8,128)(2,1)} fusion(bf16[512,1408]{1,0:T(8,128)(2,1)S(1)} %get-tuple-element.39, bf16[2048,5376]{1,0:T(8,128)(2,1)} %all-gather.2.cloned.1.call-done), kind=kOutput, calls=%fused_computation.51 | convolution fusion | flops 2953838592 | bytes 9306112 | tf_op jit(solution)/shard_map/dot_general | solution.py:68
  231.0 4.7 pad_maximum_fusion.1.left_ref
  235.7 2.1 pad_maximum_fusion.right_ref
  237.8 24.7 %shard_map.230 = bf16[2048,4224]{1,0:T(8,128)(2,1)} custom-call(s32[33]{0:T(128)} %constant.67.clone.select_ref, bf16[2,2048,512]{2,1,0:T(8,128)(2,1)} %pad_maximum_fusion.1.left_ref, bf16[512,4224]{1,0:T(8,128)(2,1)} %pad_maximum_fusion.right_ref), custom_call_target="tpu_custom_call" | custom-call | tf_op jit(solution)/shard_map/pallas_call | solution.py:222
  262.5 5.9 %fusion.2 = f32[512,2048]{1,0:T(8,128)S(1)} fusion(bf16[512,1408]{1,0:T(8,128)(2,1)} %get-tuple-element.40, bf16[2048,5376]{1,0:T(8,128)(2,1)} %all-gather.2.cloned.1.call-done), kind=kOutput, calls=%fused_computation.15 | convolution fusion | flops 2952790016 | bytes 11403264 | tf_op jit(solution)/shard_map/dot_general | solution.py:68
  268.5 7.4 %add_convert_fusion.1 = bf16[512,2048]{1,0:T(8,128)(2,1)} fusion(f32[512,2048]{1,0:T(8,128)S(1)} %fusion.2, bf16[512,1408]{1,0:T(8,128)(2,1)S(1)} %get-tuple-element.41, bf16[2048,5376]{1,0:T(8,128)(2,1)} %all-gather.2.cloned.1.call-done), kind=kOutput, calls=%fused_computation.42 | convolution fusion | flops 2954887168 | bytes 13500416 | tf_op jit(solution)/shard_map/dot_general | solution.py:68
  277.7 29.9 %all_to_all.68 = bf16[4,512,512]{2,1,0:T(8,128)(2,1)} all-to-all(bf16[4,512,512]{2,1,0:T(8,128)(2,1)S(1)} %bitcast.178), channel_id=1, replica_groups=mesh['row'=32,'col'=4] {'col'}, dimensions={0} | all-to-all | bytes 4194304 | tf_op jit(solution)/shard_map/all_to_all | solution.py:176
  307.6 2.4 reduce_sum.114
  311.7 4.6 all-to-all-start.5
  319.1 2.6 gather_fusion.3
  321.8 20.2 %all-to-all-done.5 = bf16[4,512,512]{1,2,0:T(8,128)(2,1)} async-done(((bf16[4,512,512]{1,2,0:T(8,128)(2,1)}), bf16[4,512,512]{1,2,0:T(8,128)(2,1)}, u32[]{:S(2)}, u32[]{:S(2)}) %all-to-all-start.5) | async-done | bytes 2097184 | tf_op jit(solution)/shard_map/all_to_all | solution.py:183
  342.0 7.2 %all-to-all-start.6 = ((bf16[32,16,512]{2,1,0:T(8,128)(2,1)}), bf16[32,16,512]{2,1,0:T(8,128)(2,1)S(1)}, u32[]{:S(2)}, u32[]{:S(2)}) async-start(bf16[32,16,512]{2,1,0:T(8,128)(2,1)} %bitcast.51), calls=%async_computation.8 | async-start | bytes 1048576 | tf_op jit(solution)/shard_map/all_to_all | solution.py:352
  349.4 3.9 fusion.21
  353.4 3.4 convert_bitcast_fusion
  356.9 4.8 fusion.35
  361.7 2.5 multiply_reduce_fusion
  364.2 2.6 multiply_convert_fusion
  370.8 3.7 fusion.50
  374.5 4.9 fusion.29
  381.0 2.5 pad_maximum_fusion.2.left_ref
  384.5 3.1 concatenate.57.right_ref
  387.6 10.0 %shard_map.231 = bf16[2048,1152]{1,0:T(8,128)(2,1)} custom-call(s32[9]{0:T(128)} %constant.68.clone.select_ref, bf16[2,2048,512]{2,1,0:T(8,128)(2,1)} %pad_maximum_fusion.2.left_ref, bf16[512,1152]{1,0:T(8,128)(2,1)} %concatenate.57.right_ref), custom_call_target="tpu_custom_call" | custom-call | tf_op jit(solution)/shard_map/pallas_call | solution.py:222
  397.6 5.8 %add_convert_fusion = bf16[512,2048]{1,0:T(8,128)(2,1)} fusion(f32[512,2048]{1,0:T(8,128)} %fusion.29, f32[512,2048]{1,0:T(8,128)} %fusion.50, bf16[512,64]{1,0:T(8,128)(2,1)S(1)} %fusion.44, bf16[2048,5376]{1,0:T(8,128)(2,1)} %all-gather.2.cloned.1.call-done), kind=kOutput, calls=%fused_computation.40 | convolution fusion | flops 137363456 | bytes 11075584 | tf_op jit(solution)/shard_map/dot_general | solution.py:68
  403.5 3.2 copy.177
  406.6 4.5 all-to-all-start.7
  411.9 3.8 sort.47
  415.6 2.5 convert_element_type.186
  418.2 19.9 %all-to-all-done.7 = bf16[4,512,512]{2,1,0:T(8,128)(2,1)} async-done(((bf16[4,512,512]{2,1,0:T(8,128)(2,1)}), bf16[4,512,512]{2,1,0:T(8,128)(2,1)}, u32[]{:S(2)}, u32[]{:S(2)}) %all-to-all-start.7) | async-done | bytes 2097184 | tf_op jit(solution)/shard_map/all_to_all | solution.py:176
  438.1 2.0 convert_reduce_fusion
  442.7 3.3 all-to-all-start.8
  446.1 5.2 %all-to-all-done.8 = f32[4,1,1024]{2,1,0:T(1,128)S(1)} async-done(((f32[4,1,1024]{2,1,0:T(1,128)}), f32[4,1,1024]{2,1,0:T(1,128)S(1)}, u32[]{:S(2)}, u32[]{:S(2)}) %all-to-all-start.8) | async-done | bytes 16416 | tf_op jit(solution)/shard_map/all_to_all | solution.py:183
  453.4 2.0 gather_fusion.5
  456.6 7.2 %all-to-all-start.9 = ((bf16[32,17,512]{2,1,0:T(8,128)(2,1)}), bf16[32,17,512]{2,1,0:T(8,128)(2,1)S(1)}, u32[]{:S(2)}, u32[]{:S(2)}) async-start(bf16[32,17,512]{2,1,0:T(8,128)(2,1)} %pad_maximum_fusion.4), calls=%async_computation.11 | async-start | bytes 1572864 | tf_op jit(solution)/shard_map/all_to_all | solution.py:394
  463.8 2.6 gather_fusion.4
  467.5 10.9 %all-to-all-done.9 = bf16[32,17,512]{2,1,0:T(8,128)(2,1)S(1)} async-done(((bf16[32,17,512]{2,1,0:T(8,128)(2,1)}), bf16[32,17,512]{2,1,0:T(8,128)(2,1)S(1)}, u32[]{:S(2)}, u32[]{:S(2)}) %all-to-all-start.9) | async-done | bytes 557088 | tf_op jit(solution)/shard_map/all_to_all | solution.py:394
  478.5 2.6 gather_fusion.6
  481.7 6.1 %reduce-scatter.8.cloned.1.call-done = bf16[64,1152]{1,0:T(8,128)(2,1)} async-done(((bf16[2048,1152]{1,0:T(8,128)(2,1)}), bf16[64,1152]{1,0:T(8,128)(2,1)}) %reduce-scatter.8.cloned.1.call-update) | async-done | bytes 147472 | tf_op jit(solution)/shard_map/reduce_scatter | solution.py:366
  (207 shorter events, 50.0 us)
Async XLA Ops:
  7.2 20.0 %copy-start.23 = (bf16[512,512]{1,0:T(8,128)(2,1)S(1)}, bf16[512,512]{1,0:T(8,128)(2,1)}, u32[]{:S(2)}) copy-start(bf16[512,512]{1,0:T(8,128)(2,1)} %param.15) | copy-start | bytes 1572868
  7.2 20.8 %copy-start.24 = (bf16[512,512]{1,0:T(8,128)(2,1)S(1)}, bf16[512,512]{1,0:T(8,128)(2,1)}, u32[]{:S(2)}) copy-start(bf16[512,512]{1,0:T(8,128)(2,1)} %param.16) | copy-start | bytes 1572868
  7.2 108.3 %all-gather.2.cloned.1.call-start = ((), (), s32[]{:S(2)}) async-start(), calls=%async_computation.13 | async-start | bytes 22708224 | tf_op jit(solution)/shard_map/all_gather | solution.py:192
  18.7 16.6 %all-to-all-start.1 = ((s32[32,16,1]{1,2,0:T(1,128)}), s32[32,16,1]{1,2,0:T(1,128)S(1)}, u32[]{:S(2)}, u32[]{:S(2)}) async-start(s32[32,16,1]{1,2,0:T(1,128)} %bitcast.3), calls=%async_computation.1 | async-start | bytes 32768 | tf_op jit(solution)/shard_map/all_to_all | solution.py:258
  35.4 34.3 %copy-start.28 = (s32[32,16,1]{1,2,0:T(1,128)}, s32[32,16,1]{1,2,0:T(1,128)S(1)}, u32[]{:S(2)}) copy-start(s32[32,16,1]{1,2,0:T(1,128)S(1)} %all-to-all-done.1) | copy-start | bytes 6148
  35.4 30.7 %all-to-all-start = ((bf16[2,512,512]{2,0,1:T(2,128)(2,1)}), bf16[2,512,512]{2,0,1:T(2,128)(2,1)S(1)}, u32[]{:S(2)}, u32[]{:S(2)}) async-start(bf16[2,512,512]{2,0,1:T(2,128)(2,1)} %bitcast.2), calls=%async_computation | async-start | bytes 2097152 | tf_op jit(solution)/shard_map/all_to_all | solution.py:255
  71.2 7.2 %copy-start.42 = (s32[512]{0:T(512)S(1)}, s32[512]{0:T(512)}, u32[]{:S(2)}) copy-start(s32[512]{0:T(512)} %param.18) | copy-start | bytes 6148
  71.2 7.7 %copy-start.38 = (f32[2048]{0:T(1024)S(1)}, f32[2048]{0:T(1024)}, u32[]{:S(2)}) copy-start(f32[2048]{0:T(1024)} %param.19) | copy-start | bytes 24580
  74.0 30.0 %all-to-all-start.2 = ((bf16[4,512,512]{1,2,0:T(8,128)(2,1)}), bf16[4,512,512]{1,2,0:T(8,128)(2,1)S(1)}, u32[]{:S(2)}, u32[]{:S(2)}) async-start(bf16[4,512,512]{1,2,0:T(8,128)(2,1)} %broadcast_in_dim.31), calls=%async_computation.2 | async-start | bytes 4194304 | tf_op jit(solution)/shard_map/all_to_all | solution.py:183
  80.0 37.9 %copy-start.39 = (f32[512]{0:T(512)}, f32[512]{0:T(512)S(1)}, u32[]{:S(2)}) copy-start(f32[512]{0:T(512)S(1)} %fusion.75) | copy-start | bytes 6148
  80.3 49.4 %copy-start.19 = (f32[512,32]{0,1:T(8,128)}, f32[512,32]{0,1:T(8,128)S(1)}, u32[]{:S(2)}) copy-start(f32[512,32]{0,1:T(8,128)S(1)} %get-tuple-element.61) | copy-start | bytes 196612
  80.4 49.4 %copy-start.21 = (f32[512,32]{0,1:T(8,128)}, f32[512,32]{0,1:T(8,128)S(1)}, u32[]{:S(2)}) copy-start(f32[512,32]{0,1:T(8,128)S(1)} %get-tuple-element.62) | copy-start | bytes 196612
  104.0 7.8 %copy-start.41 = (f32[4,512]{1,0:T(4,128)S(1)}, f32[4,512]{1,0:T(4,128)}, u32[]{:S(2)}) copy-start(f32[4,512]{1,0:T(4,128)} %mul.298) | copy-start | bytes 24580
  106.6 37.2 %all-to-all-start.3 = ((bf16[4,512,512]{1,2,0:T(8,128)(2,1)}), bf16[4,512,512]{1,2,0:T(8,128)(2,1)}, u32[]{:S(2)}, u32[]{:S(2)}) async-start(bf16[4,512,512]{1,2,0:T(8,128)(2,1)} %broadcast_in_dim.33), calls=%async_computation.3 | async-start | bytes 4194304 | tf_op jit(solution)/shard_map/all_to_all | solution.py:183
  111.0 90.6 %all-reduce.3.cloned.1.call-start = ((), (), s32[]{:S(2)}) async-start(), calls=%async_computation.14 | async-start | bytes 4194304 | tf_op jit(solution)/shard_map/psum | solution.py:301
  111.8 1.9 copy-start.36
  113.7 4.3 copy-start.48
  119.2 10.8 %copy-start.11 = (bf16[512,32]{1,0:T(8,128)(2,1)}, bf16[512,32]{1,0:T(8,128)(2,1)S(1)}, u32[]{:S(2)}) copy-start(bf16[512,32]{1,0:T(8,128)(2,1)S(1)} %get-tuple-element.55) | copy-start | bytes 98308
  119.2 10.8 %copy-start.13 = (bf16[512,32]{1,0:T(8,128)(2,1)}, bf16[512,32]{1,0:T(8,128)(2,1)S(1)}, u32[]{:S(2)}) copy-start(bf16[512,32]{1,0:T(8,128)(2,1)S(1)} %get-tuple-element.56) | copy-start | bytes 98308
  129.9 1.5 copy-start.15
  129.9 1.5 copy-start.17
  131.5 5.3 %copy-start = (f32[8,512,512]{1,2,0:T(8,128)}, f32[8,512,512]{1,2,0:T(8,128)S(1)}, u32[]{:S(2)}) copy-start(f32[8,512,512]{1,2,0:T(8,128)S(1)} %get-tuple-element.66) | copy-start | bytes 25165828
  131.5 3.2 copy-start.4
  134.6 3.7 copy-start.34
  136.8 1.6 copy-start.32
  143.3 132.6 %reduce-scatter.4.cloned.1.call-start = ((), (), s32[]{:S(2)}) async-start(), calls=%async_computation.15 | async-start | bytes 2621440 | tf_op jit(solution)/shard_map/reduce_scatter | solution.py:311
  152.1 52.0 %copy-start.30 = (f32[2048]{0:T(1024)S(1)}, f32[2048]{0:T(1024)}, u32[]{:S(2)}) copy-start(f32[2048]{0:T(1024)} %param.24) | copy-start | bytes 24580
  201.7 2.5 copy-start.1
  204.2 2.7 copy-start.43
  206.9 6.4 %copy-start.3 = (bf16[512,2048]{0,1:T(8,128)(2,1)}, bf16[512,2048]{0,1:T(8,128)(2,1)S(1)}, u32[]{:S(2)}) copy-start(bf16[512,2048]{0,1:T(8,128)(2,1)S(1)} %get-tuple-element.43) | copy-start | bytes 6291460
  206.9 6.4 %copy-start.50 = (f32[512,1408]{1,0:T(8,128)S(1)}, f32[512,1408]{1,0:T(8,128)}, u32[]{:S(2)}) copy-start(f32[512,1408]{1,0:T(8,128)} %fusion.12) | copy-start | bytes 8650756
  222.3 1.1 copy-start.9
  230.7 172.7 %reduce-scatter.6.cloned.1.call-start = ((), (), s32[]{:S(2)}) async-start(), calls=%async_computation.16 | async-start | bytes 17842176 | tf_op jit(solution)/shard_map/reduce_scatter | solution.py:329
  231.0 4.7 copy-start.8
  231.0 4.7 copy-start.10
  309.9 6.4 %copy-start.29 = (s32[32,16,1]{1,2,0:T(1,128)S(1)}, s32[32,16,1]{1,2,0:T(1,128)}, u32[]{:S(2)}) copy-start(s32[32,16,1]{1,2,0:T(1,128)} %copy-done.28) | copy-start | bytes 6148
  310.2 6.3 %copy-start.27 = (bf16[8,512,64]{1,2,0:T(8,128)(2,1)S(1)}, bf16[8,512,64]{1,2,0:T(8,128)(2,1)}, u32[]{:S(2)}) copy-start(bf16[8,512,64]{1,2,0:T(8,128)(2,1)} %copy-done.26) | copy-start | bytes 1572868
  310.2 7.3 %copy-start.35 = (f32[8,512]{1,0:T(8,128)S(1)}, f32[8,512]{1,0:T(8,128)}, u32[]{:S(2)}) copy-start(f32[8,512]{1,0:T(8,128)} %copy-done.34) | copy-start | bytes 49156
  311.7 5.8 %copy-start.25 = (bf16[512,512]{0,1:T(8,128)(2,1)S(1)}, bf16[512,512]{0,1:T(8,128)(2,1)}, u32[]{:S(2)}) copy-start(bf16[512,512]{0,1:T(8,128)(2,1)} %reduce-scatter.4.cloned.1.call-done) | copy-start | bytes 1572868
  311.7 30.3 %all-to-all-start.5 = ((bf16[4,512,512]{1,2,0:T(8,128)(2,1)}), bf16[4,512,512]{1,2,0:T(8,128)(2,1)}, u32[]{:S(2)}, u32[]{:S(2)}) async-start(bf16[4,512,512]{1,2,0:T(8,128)(2,1)} %broadcast_in_dim.36), calls=%async_computation.6 | async-start | bytes 4194304 | tf_op jit(solution)/shard_map/all_to_all | solution.py:183
  317.5 31.9 %copy-start.31 = (f32[2048]{0:T(1024)S(1)}, f32[2048]{0:T(1024)}, u32[]{:S(2)}) copy-start(f32[2048]{0:T(1024)} %param.24) | copy-start | bytes 24580
  317.5 31.9 %copy-start.44 = (f32[512]{0:T(512)S(1)}, f32[512]{0:T(512)}, u32[]{:S(2)}) copy-start(f32[512]{0:T(512)} %copy-done.43) | copy-start | bytes 6148
  342.0 61.5 %all-to-all-start.6 = ((bf16[32,16,512]{2,1,0:T(8,128)(2,1)}), bf16[32,16,512]{2,1,0:T(8,128)(2,1)S(1)}, u32[]{:S(2)}, u32[]{:S(2)}) async-start(bf16[32,16,512]{2,1,0:T(8,128)(2,1)} %bitcast.51), calls=%async_computation.8 | async-start | bytes 1048576 | tf_op jit(solution)/shard_map/all_to_all | solution.py:352
  349.1 138.7 %reduce-scatter.8.cloned.1.call-start = ((), (), s32[]{:S(2)}) async-start(), calls=%async_computation.17 | async-start | bytes 4866048 | tf_op jit(solution)/shard_map/reduce_scatter | solution.py:366
  349.4 4.0 copy-start.2
  353.4 8.3 %slice-start = ((s8[8388608]{0:T(1024)(128)(4,1)}), s8[4194304]{0:T(1024)(128)(4,1)S(1)}, s32[]{:S(2)}) async-start(s8[8388608]{0:T(1024)(128)(4,1)} %bitcast.169), calls=%async_computation.18 | async-start | bytes 8388608
  353.4 8.3 %slice-start.1 = ((s8[8388608]{0:T(1024)(128)(4,1)}), s8[4194304]{0:T(1024)(128)(4,1)S(1)}, s32[]{:S(2)}) async-start(s8[8388608]{0:T(1024)(128)(4,1)} %bitcast.169), calls=%async_computation.19 | async-start | bytes 8388608
  356.9 4.8 copy-start.6
  356.9 4.8 copy-start.33
  364.2 2.6 copy-start.16
  364.2 2.6 copy-start.18
  366.9 1.3 copy-start.40
  366.9 1.3 copy-start.49
  366.9 2.6 copy-start.12
  366.9 2.6 copy-start.14
  368.1 2.4 copy-start.20
  368.2 2.4 copy-start.22
  379.4 1.6 copy-start.5
  403.5 8.4 %copy-start.46 = (s32[512]{0:T(512)S(1)}, s32[512]{0:T(512)}, u32[]{:S(2)}) copy-start(s32[512]{0:T(512)} %copy-done.45) | copy-start | bytes 6148
  406.6 31.5 %all-to-all-start.7 = ((bf16[4,512,512]{2,1,0:T(8,128)(2,1)}), bf16[4,512,512]{2,1,0:T(8,128)(2,1)}, u32[]{:S(2)}, u32[]{:S(2)}) async-start(bf16[4,512,512]{2,1,0:T(8,128)(2,1)} %bitcast.177), calls=%async_computation.9 | async-start | bytes 4194304 | tf_op jit(solution)/shard_map/all_to_all | solution.py:176
  418.2 22.3 %copy-start.37 = (f32[512]{0:T(512)S(1)}, f32[512]{0:T(512)}, u32[]{:S(2)}) copy-start(f32[512]{0:T(512)} %copy-done.36) | copy-start | bytes 6148
  442.7 8.6 %all-to-all-start.8 = ((f32[4,1,1024]{2,1,0:T(1,128)}), f32[4,1,1024]{2,1,0:T(1,128)S(1)}, u32[]{:S(2)}, u32[]{:S(2)}) async-start(f32[4,1,1024]{2,1,0:T(1,128)} %broadcast_in_dim.38), calls=%async_computation.10 | async-start | bytes 32768 | tf_op jit(solution)/shard_map/all_to_all | solution.py:183
  455.4 11.1 %copy-start.7 = (bf16[64,4224]{1,0:T(8,128)(2,1)S(1)}, bf16[64,4224]{1,0:T(8,128)(2,1)}, u32[]{:S(2)}) copy-start(bf16[64,4224]{1,0:T(8,128)(2,1)} %reduce-scatter.6.cloned.1.call-done) | copy-start | bytes 1622020
  456.6 21.8 %all-to-all-start.9 = ((bf16[32,17,512]{2,1,0:T(8,128)(2,1)}), bf16[32,17,512]{2,1,0:T(8,128)(2,1)S(1)}, u32[]{:S(2)}, u32[]{:S(2)}) async-start(bf16[32,17,512]{2,1,0:T(8,128)(2,1)} %pad_maximum_fusion.4), calls=%async_computation.11 | async-start | bytes 1572864 | tf_op jit(solution)/shard_map/all_to_all | solution.py:394
  (3 other events, 1.9 us)
Sparse Core Ops, SparseCore 0:
  10.3 94.5 all-gather.1
  143.4 58.1 all-reduce.2
  230.9 29.4 reduce-scatter.3
  276.0 122.5 reduce-scatter.5
  403.6 84.2 reduce-scatter.7
